TPU v7x, 128 devices: a whole 4x4x4 slice. The times are simulated.
128 devices in a mesh: row: 16 (over x, z_hi, core), col: 8 (over z_lo, y).
Axes of the slice: x: 4, y: 4, z: 4 (z_hi: 2, z_lo: 2; z = z_hi * 2 + z_lo), core: 2. Of those that a mesh axis runs over, the one named last changes fastest.
Arguments:
- left: bfloat16 [128, 32768], P('col', 'row'), may hold values from -15 to 15
- right: bfloat16 [128, 32768], P('row', 'col'), may hold values from -15 to 15
- weight: bfloat16 [1024, 128], replicated, may hold values from -0.1875 to 0.1875
- bias: float32 [128], replicated, may hold values from -3 to 3
- cotangent: bfloat16 [1024, 1024, 128], P('row', 'col'), may hold values from -0.1796875 to 0.1796875
Outputs:
- pair_update: bfloat16 [1024, 1024, 128], P('row', 'col')
- grad_left: bfloat16 [128, 32768], P('col', 'row')
- grad_right: bfloat16 [128, 32768], P('row', 'col')
- grad_weight: float32 [1024, 128], replicated
- grad_bias: float32 [128], replicated
All inputs are finite; a program needn't handle non-finite values.
Results may differ from a plain program's by a relative error of at most 0.005.
Values may be sent and summed in bfloat16 or wider, within the bound.
No kernel may reach another device: no remote copies, remote signals or barrier semaphores. Data moves between devices by JAX's collectives and lax.ppermute only.
A program may use at most 128 MiB of HBM per device.

v0:
```python
import jax
import jax.numpy as jnp
from jax import lax
from jax.sharding import PartitionSpec as P

CL = 32
CP = 128


def shards(left, right, weight, bias, cotangent):
    left_full = lax.all_gather(left, "col", axis=0, tiled=True)
    right_full = lax.all_gather(right, "row", axis=0, tiled=True)
    seqs = left_full.shape[0]
    rows_i = left.shape[1] // CL
    cols_j = right.shape[1] // CL
    block = min(8, rows_i)
    nblock = rows_i // block
    scale = 1.0 / seqs
    weight_cube = weight.reshape(CL, CL, CP)
    right_view = right_full.reshape(seqs, cols_j, CL)

    def step(carry, index):
        grad_w, grad_b, grad_r = carry
        lblock = lax.dynamic_slice_in_dim(left_full, index * block * CL, block * CL, 1)
        raw = lax.dot_general(
            lblock, right_full, (((0,), (0,)), ((), ())), preferred_element_type=jnp.float32
        )
        outer = (raw * scale).astype(jnp.bfloat16).reshape(block, CL, cols_j, CL)
        partial_pair = lax.dot_general(
            outer, weight_cube, (((3,), (1,)), ((1,), (0,))), preferred_element_type=jnp.float32
        )
        pair = (jnp.sum(partial_pair, axis=0) + bias).astype(jnp.bfloat16)
        dpair = lax.dynamic_slice_in_dim(cotangent, index * block, block, 0)
        grad_outer = lax.dot_general(
            weight_cube, dpair, (((2,), (2,)), ((), ())), preferred_element_type=jnp.float32
        ).astype(jnp.bfloat16)
        grad_w = grad_w + lax.dot_general(
            outer, dpair, (((0, 2), (0, 1)), ((), ())), preferred_element_type=jnp.float32
        )
        grad_b = grad_b + jnp.sum(dpair.astype(jnp.float32), axis=(0, 1))
        grad_l = (
            lax.dot_general(
                grad_outer,
                right_view,
                (((1, 3), (2, 1)), ((), ())),
                preferred_element_type=jnp.float32,
            )
            * scale
        )
        left_view = lblock.reshape(seqs, block, CL)
        grad_r = (
            grad_r
            + lax.dot_general(
                grad_outer,
                left_view,
                (((0, 2), (2, 1)), ((), ())),
                preferred_element_type=jnp.float32,
            )
            * scale
        )
        return ((grad_w, grad_b, grad_r), (pair, grad_l))

    start = (
        jnp.zeros((CL, CL, CP), jnp.float32),
        jnp.zeros((CP,), jnp.float32),
        jnp.zeros((CL, cols_j, seqs), jnp.float32),
    )
    (grad_w, grad_b, grad_r), stacked = lax.scan(step, start, jnp.arange(nblock, dtype=jnp.int32))
    pair_update = stacked[0].reshape(rows_i, cols_j, CP)
    grad_lpart = stacked[1].transpose(3, 0, 2, 1).reshape(seqs, rows_i * CL)
    grad_left = lax.psum_scatter(grad_lpart, "col", scatter_dimension=0, tiled=True).astype(
        jnp.bfloat16
    )
    grad_rows = grad_r.transpose(2, 1, 0).reshape(seqs, cols_j * CL)
    grad_right = lax.psum_scatter(grad_rows, "row", scatter_dimension=0, tiled=True).astype(
        jnp.bfloat16
    )
    grad_w, grad_b = lax.psum((grad_w.reshape(CL * CL, CP), grad_b), ("row", "col"))
    return (pair_update, grad_left, grad_right, grad_w, grad_b)


def solution(mesh):
    placed = (P("col", "row"), P("row", "col"), P(), P(), P("row", "col", None))
    return jax.shard_map(
        shards,
        mesh=mesh,
        in_specs=placed,
        out_specs=(P("row", "col", None), P("col", "row"), P("row", "col"), P(), P()),
        check_vma=False,
    )
```

profile of v0, /device:TPU:1, one launch (start us, length us, event | category | flops | bytes accessed | tf_op | source)
XLA Modules:
  0.0 563.9 jit_solution(295560597329324322)
XLA Ops:
  8.0 25.0 %all_gather.6 = bf16[128,2048]{1,0:T(8,128)(2,1)S(1)} all-gather(bf16[16,2048]{1,0:T(8,128)(2,1)} %param.7), channel_id=1, replica_groups=mesh['row'=16,'col'=8] {'col'}, dimensions={0}, use_global_device_ids=true | all-gather | bytes 589824 | tf_op jit(solution)/shard_map/all_gather | solution.py:11
  33.0 25.9 %all-gather.2.cloned.1.call-done = bf16[128,4096]{1,0:T(8,128)(2,1)} async-done(((bf16[8,4096]{1,0:T(8,128)(2,1)}), bf16[128,4096]{1,0:T(8,128)(2,1)}) %all-gather.2.cloned.1.call-update) | async-done | bytes 1048592 | tf_op jit(solution)/shard_map/all_gather | solution.py:12
  62.3 228.1 %while.21 = (s32[]{:T(128)}, f32[32,32,128]{2,1,0:T(8,128)}, f32[128]{0:T(128)S(1)}, f32[32,128,128]{2,1,0:T(8,128)}, bf16[8,8,128,128]{3,2,1,0:T(8,128)(2,1)}, ...) while((s32[]{:T(128)}, f32[32,32,128]{2,1,0:T(8,128)}, ...), condition=%wide.region_2.0_spmd.clone, body=%wide.region_0.2_spmd.clone.sunk | while | flops 1616150656 | bytes 66325480 | solution.py:68
  73.6 8.0 %reshape.66 = bf16[8,32,128,32]{3,2,1,0:T(8,128)(2,1)} reshape(bf16[256,4096]{1,0:T(8,128)(2,1)S(1)} %fusion.67) | data formatting | bytes 4194304 | tf_op jit(solution)/shard_map/while/body/eval_jaxpr/reshape | solution.py:28
  81.6 6.7 %fusion.68 = f32[32,32,128]{2,1,0:T(8,128)} fusion(bf16[8,32,128,32]{3,2,1,0:T(8,128)(2,1)} %reshape.66, f32[32,32,128]{2,1,0:T(8,128)} %get-tuple-element.378, pred[]{:T(512)S(6)} %compare.3, bf16[64,128,128]{2,1,0:T(8,128)(2,1)} %get-tuple-element.405, s32[]{:T(128)S(6)} %select_n.17), kind=kOutput, calls=%fused_computation.11.clone.1 | convolution fusion | flops 268697600 | bytes 9699333 | tf_op jit(solution)/shard_map/while/body/eval_jaxpr/dot_general | solution.py:37
  88.3 2.4 fusion.71
  102.0 8.0 %reshape.66 = bf16[8,32,128,32]{3,2,1,0:T(8,128)(2,1)} reshape(bf16[256,4096]{1,0:T(8,128)(2,1)S(1)} %fusion.67) | data formatting | bytes 4194304 | tf_op jit(solution)/shard_map/while/body/eval_jaxpr/reshape | solution.py:28
  110.1 6.8 %fusion.68 = f32[32,32,128]{2,1,0:T(8,128)} fusion(bf16[8,32,128,32]{3,2,1,0:T(8,128)(2,1)} %reshape.66, f32[32,32,128]{2,1,0:T(8,128)} %get-tuple-element.378, pred[]{:T(512)S(6)} %compare.3, bf16[64,128,128]{2,1,0:T(8,128)(2,1)} %get-tuple-element.405, s32[]{:T(128)S(6)} %select_n.17), kind=kOutput, calls=%fused_computation.11.clone.1 | convolution fusion | flops 268697600 | bytes 9699333 | tf_op jit(solution)/shard_map/while/body/eval_jaxpr/dot_general | solution.py:37
  116.9 2.4 fusion.71
  130.5 8.0 %reshape.66 = bf16[8,32,128,32]{3,2,1,0:T(8,128)(2,1)} reshape(bf16[256,4096]{1,0:T(8,128)(2,1)S(1)} %fusion.67) | data formatting | bytes 4194304 | tf_op jit(solution)/shard_map/while/body/eval_jaxpr/reshape | solution.py:28
  138.6 6.8 %fusion.68 = f32[32,32,128]{2,1,0:T(8,128)} fusion(bf16[8,32,128,32]{3,2,1,0:T(8,128)(2,1)} %reshape.66, f32[32,32,128]{2,1,0:T(8,128)} %get-tuple-element.378, pred[]{:T(512)S(6)} %compare.3, bf16[64,128,128]{2,1,0:T(8,128)(2,1)} %get-tuple-element.405, s32[]{:T(128)S(6)} %select_n.17), kind=kOutput, calls=%fused_computation.11.clone.1 | convolution fusion | flops 268697600 | bytes 9699333 | tf_op jit(solution)/shard_map/while/body/eval_jaxpr/dot_general | solution.py:37
  145.4 2.4 fusion.71
  159.0 8.0 %reshape.66 = bf16[8,32,128,32]{3,2,1,0:T(8,128)(2,1)} reshape(bf16[256,4096]{1,0:T(8,128)(2,1)S(1)} %fusion.67) | data formatting | bytes 4194304 | tf_op jit(solution)/shard_map/while/body/eval_jaxpr/reshape | solution.py:28
  167.1 6.8 %fusion.68 = f32[32,32,128]{2,1,0:T(8,128)} fusion(bf16[8,32,128,32]{3,2,1,0:T(8,128)(2,1)} %reshape.66, f32[32,32,128]{2,1,0:T(8,128)} %get-tuple-element.378, pred[]{:T(512)S(6)} %compare.3, bf16[64,128,128]{2,1,0:T(8,128)(2,1)} %get-tuple-element.405, s32[]{:T(128)S(6)} %select_n.17), kind=kOutput, calls=%fused_computation.11.clone.1 | convolution fusion | flops 268697600 | bytes 9699333 | tf_op jit(solution)/shard_map/while/body/eval_jaxpr/dot_general | solution.py:37
  173.9 2.4 fusion.71
  187.6 8.0 %reshape.66 = bf16[8,32,128,32]{3,2,1,0:T(8,128)(2,1)} reshape(bf16[256,4096]{1,0:T(8,128)(2,1)S(1)} %fusion.67) | data formatting | bytes 4194304 | tf_op jit(solution)/shard_map/while/body/eval_jaxpr/reshape | solution.py:28
  195.6 6.8 %fusion.68 = f32[32,32,128]{2,1,0:T(8,128)} fusion(bf16[8,32,128,32]{3,2,1,0:T(8,128)(2,1)} %reshape.66, f32[32,32,128]{2,1,0:T(8,128)} %get-tuple-element.378, pred[]{:T(512)S(6)} %compare.3, bf16[64,128,128]{2,1,0:T(8,128)(2,1)} %get-tuple-element.405, s32[]{:T(128)S(6)} %select_n.17), kind=kOutput, calls=%fused_computation.11.clone.1 | convolution fusion | flops 268697600 | bytes 9699333 | tf_op jit(solution)/shard_map/while/body/eval_jaxpr/dot_general | solution.py:37
  202.4 2.4 fusion.71
  216.1 8.0 %reshape.66 = bf16[8,32,128,32]{3,2,1,0:T(8,128)(2,1)} reshape(bf16[256,4096]{1,0:T(8,128)(2,1)S(1)} %fusion.67) | data formatting | bytes 4194304 | tf_op jit(solution)/shard_map/while/body/eval_jaxpr/reshape | solution.py:28
  224.1 6.8 %fusion.68 = f32[32,32,128]{2,1,0:T(8,128)} fusion(bf16[8,32,128,32]{3,2,1,0:T(8,128)(2,1)} %reshape.66, f32[32,32,128]{2,1,0:T(8,128)} %get-tuple-element.378, pred[]{:T(512)S(6)} %compare.3, bf16[64,128,128]{2,1,0:T(8,128)(2,1)} %get-tuple-element.405, s32[]{:T(128)S(6)} %select_n.17), kind=kOutput, calls=%fused_computation.11.clone.1 | convolution fusion | flops 268697600 | bytes 9699333 | tf_op jit(solution)/shard_map/while/body/eval_jaxpr/dot_general | solution.py:37
  230.9 2.4 fusion.71
  244.6 8.0 %reshape.66 = bf16[8,32,128,32]{3,2,1,0:T(8,128)(2,1)} reshape(bf16[256,4096]{1,0:T(8,128)(2,1)S(1)} %fusion.67) | data formatting | bytes 4194304 | tf_op jit(solution)/shard_map/while/body/eval_jaxpr/reshape | solution.py:28
  252.7 6.8 %fusion.68 = f32[32,32,128]{2,1,0:T(8,128)} fusion(bf16[8,32,128,32]{3,2,1,0:T(8,128)(2,1)} %reshape.66, f32[32,32,128]{2,1,0:T(8,128)} %get-tuple-element.378, pred[]{:T(512)S(6)} %compare.3, bf16[64,128,128]{2,1,0:T(8,128)(2,1)} %get-tuple-element.405, s32[]{:T(128)S(6)} %select_n.17), kind=kOutput, calls=%fused_computation.11.clone.1 | convolution fusion | flops 268697600 | bytes 9699333 | tf_op jit(solution)/shard_map/while/body/eval_jaxpr/dot_general | solution.py:37
  259.5 2.4 fusion.71
  273.2 8.0 %reshape.66 = bf16[8,32,128,32]{3,2,1,0:T(8,128)(2,1)} reshape(bf16[256,4096]{1,0:T(8,128)(2,1)S(1)} %fusion.67) | data formatting | bytes 4194304 | tf_op jit(solution)/shard_map/while/body/eval_jaxpr/reshape | solution.py:28
  281.2 6.8 %fusion.68 = f32[32,32,128]{2,1,0:T(8,128)} fusion(bf16[8,32,128,32]{3,2,1,0:T(8,128)(2,1)} %reshape.66, f32[32,32,128]{2,1,0:T(8,128)} %get-tuple-element.378, pred[]{:T(512)S(6)} %compare.3, bf16[64,128,128]{2,1,0:T(8,128)(2,1)} %get-tuple-element.405, s32[]{:T(128)S(6)} %select_n.17), kind=kOutput, calls=%fused_computation.11.clone.1 | convolution fusion | flops 268697600 | bytes 9699333 | tf_op jit(solution)/shard_map/while/body/eval_jaxpr/dot_general | solution.py:37
  288.0 2.4 fusion.71
  290.5 2.5 copy.49
  293.1 2.8 copy.40
  298.4 64.8 %psum.15 = f32[128]{0:T(128)} all-reduce(f32[128]{0:T(128)S(1)} %get-tuple-element.174), channel_id=1, replica_groups=mesh['row'=16,'col'=8] {'row','col'}, use_global_device_ids=true, to_apply=%region_6.7 | all-reduce | flops 128 | bytes 1024 | tf_op jit(solution)/shard_map/psum | solution.py:78
  365.2 37.6 %reduce-scatter.9.cloned.1.call-done = f32[8,4096]{1,0:T(8,128)} async-done(((f32[128,4096]{1,0:T(8,128)}), f32[8,4096]{1,0:T(8,128)}) %reduce-scatter.9.cloned.1.call-update) | async-done | bytes 131088
  405.2 150.3 %all-reduce.2.cloned.1.call-done = f32[1024,128]{1,0:T(8,128)} async-done(((f32[1024,128]{1,0:T(8,128)}), f32[1024,128]{1,0:T(8,128)}) %all-reduce.2.cloned.1.call-update) | async-done | bytes 524304 | tf_op jit(solution)/shard_map/psum | solution.py:78
  (205 shorter events, 91.8 us)
Async XLA Ops:
  7.2 51.7 %all-gather.2.cloned.1.call-start = ((), (), s32[]{:S(2)}) async-start(), calls=%async_computation.2 | async-start | bytes 1114112 | tf_op jit(solution)/shard_map/all_gather | solution.py:12
  7.9 355.3 %reduce-scatter.7.cloned.1.call-start = ((), (), s32[]{:S(2)}) async-start(), calls=%async_computation.4 | async-start | bytes 1179648
  33.0 29.3 %copy-start.2 = (bf16[1024,128]{1,0:T(8,128)(2,1)S(1)}, bf16[1024,128]{1,0:T(8,128)(2,1)}, u32[]{:S(2)}) copy-start(bf16[1024,128]{1,0:T(8,128)(2,1)} %param.9) | copy-start | bytes 786436
  33.0 29.3 %copy-start.8 = (f32[128]{0:T(128)S(1)}, f32[128]{0:T(128)}, u32[]{:S(2)}) copy-start(f32[128]{0:T(128)} %param.10) | copy-start | bytes 1540
  58.9 3.4 copy-start.1
  62.3 3.2 copy-start.5
  66.3 1.8 copy-start.7
  81.6 6.7 %copy-start = (bf16[8,32,128,32]{3,2,1,0:T(8,128)(2,1)S(1)}, bf16[8,32,128,32]{3,2,1,0:T(8,128)(2,1)}, u32[]{:S(2)}) copy-start(bf16[8,32,128,32]{3,2,1,0:T(8,128)(2,1)} %reshape.66) | copy-start | bytes 6291460 | tf_op jit(solution)/shard_map/while
  88.3 2.4 copy-start.6
  90.8 3.2 copy-start.5
  110.1 6.8 %copy-start = (bf16[8,32,128,32]{3,2,1,0:T(8,128)(2,1)S(1)}, bf16[8,32,128,32]{3,2,1,0:T(8,128)(2,1)}, u32[]{:S(2)}) copy-start(bf16[8,32,128,32]{3,2,1,0:T(8,128)(2,1)} %reshape.66) | copy-start | bytes 6291460 | tf_op jit(solution)/shard_map/while
  116.8 2.4 copy-start.6
  119.3 3.2 copy-start.5
  138.6 6.8 %copy-start = (bf16[8,32,128,32]{3,2,1,0:T(8,128)(2,1)S(1)}, bf16[8,32,128,32]{3,2,1,0:T(8,128)(2,1)}, u32[]{:S(2)}) copy-start(bf16[8,32,128,32]{3,2,1,0:T(8,128)(2,1)} %reshape.66) | copy-start | bytes 6291460 | tf_op jit(solution)/shard_map/while
  145.4 2.4 copy-start.6
  147.8 3.2 copy-start.5
  167.1 6.8 %copy-start = (bf16[8,32,128,32]{3,2,1,0:T(8,128)(2,1)S(1)}, bf16[8,32,128,32]{3,2,1,0:T(8,128)(2,1)}, u32[]{:S(2)}) copy-start(bf16[8,32,128,32]{3,2,1,0:T(8,128)(2,1)} %reshape.66) | copy-start | bytes 6291460 | tf_op jit(solution)/shard_map/while
  173.9 2.4 copy-start.6
  176.3 3.2 copy-start.5
  195.6 6.8 %copy-start = (bf16[8,32,128,32]{3,2,1,0:T(8,128)(2,1)S(1)}, bf16[8,32,128,32]{3,2,1,0:T(8,128)(2,1)}, u32[]{:S(2)}) copy-start(bf16[8,32,128,32]{3,2,1,0:T(8,128)(2,1)} %reshape.66) | copy-start | bytes 6291460 | tf_op jit(solution)/shard_map/while
  202.4 2.4 copy-start.6
  204.9 3.2 copy-start.5
  224.1 6.8 %copy-start = (bf16[8,32,128,32]{3,2,1,0:T(8,128)(2,1)S(1)}, bf16[8,32,128,32]{3,2,1,0:T(8,128)(2,1)}, u32[]{:S(2)}) copy-start(bf16[8,32,128,32]{3,2,1,0:T(8,128)(2,1)} %reshape.66) | copy-start | bytes 6291460 | tf_op jit(solution)/shard_map/while
  230.9 2.4 copy-start.6
  233.4 3.2 copy-start.5
  252.7 6.8 %copy-start = (bf16[8,32,128,32]{3,2,1,0:T(8,128)(2,1)S(1)}, bf16[8,32,128,32]{3,2,1,0:T(8,128)(2,1)}, u32[]{:S(2)}) copy-start(bf16[8,32,128,32]{3,2,1,0:T(8,128)(2,1)} %reshape.66) | copy-start | bytes 6291460 | tf_op jit(solution)/shard_map/while
  259.5 2.4 copy-start.6
  261.9 3.2 copy-start.5
  281.2 6.8 %copy-start = (bf16[8,32,128,32]{3,2,1,0:T(8,128)(2,1)S(1)}, bf16[8,32,128,32]{3,2,1,0:T(8,128)(2,1)}, u32[]{:S(2)}) copy-start(bf16[8,32,128,32]{3,2,1,0:T(8,128)(2,1)} %reshape.66) | copy-start | bytes 6291460 | tf_op jit(solution)/shard_map/while
  288.0 2.4 copy-start.6
  293.0 109.8 %reduce-scatter.9.cloned.1.call-start = ((), (), s32[]{:S(2)}) async-start(), calls=%async_computation.5 | async-start | bytes 2228224
  297.8 257.8 %all-reduce.2.cloned.1.call-start = ((), (), s32[]{:S(2)}) async-start(), calls=%async_computation.3 | async-start | bytes 1048576 | tf_op jit(solution)/shard_map/psum | solution.py:78
  (23 other events, 35.9 us)
Sparse Core Ops, SparseCore 0:
  10.4 48.4 all-gather.1
  293.1 32.8 reduce-scatter.6
  330.0 72.8 reduce-scatter.8
  408.0 147.4 all-reduce.1
where the time goes:
time: 565 us; the launch traced here: 564 us
  waiting for transfers between devices  215 us (38%)
  matrix products  119 us (21%)
  local copies, waits for them, and re-layouts  106 us (19%)
  blocking collectives  89.9 us (16%)
  between operations  13.8 us (2%)
  loops' own time  11.1 us (2%)
  other arithmetic  8.94 us (2%)
    psum x1, waiting for transfers between devices, shards(): lax.psum((grad_w.reshape(CL * CL, CP), grad_b), ('row', 'col'))  150 us
    psum x1, blocking collectives, shards(): lax.psum((grad_w.reshape(CL * CL, CP), grad_b), ('row', 'col'))  64.8 us
    reshape x8, local copies, waits for them, and re-layouts, step(): outer = (raw * scale).astype(jnp.bfloat16).reshape(block, CL, cols_j, CL)  64.4 us
    dot_general x8, matrix products, step(): lax.dot_general(outer, dpair, (((0, 2), (0, 1)), ((), ())), preferred_ele...  54.2 us
    unnamed x6, waiting for transfers between devices  38.9 us
    all_gather x1, waiting for transfers between devices, shards(): right_full = lax.all_gather(right, 'row', axis=0, tiled=True)  25.9 us
    all_gather x1, blocking collectives, shards(): left_full = lax.all_gather(left, 'col', axis=0, tiled=True)  25 us
    dot_general x8, matrix products, step(): lax.dot_general(outer, weight_cube, (((3,), (1,)), ((1,), (0,))), preferr...  19.5 us
  transfers between devices with their start and end apart: 4, of which 3 were waited for; matrix products, arithmetic and copies ran while one was open for 2% of the time, Pallas kernels for 0%

commit v1 on v0

v1 whole, which is shorter than its diff:
```python
import jax
import jax.numpy as jnp
from jax import lax
from jax.experimental import pallas as pl
from jax.experimental.pallas import tpu as pltpu
from jax.sharding import PartitionSpec as P

CL = 32
CP = 128
IB = 8
EB = 8
BF = jnp.bfloat16
F32 = jnp.float32


def dot(a, b, ca, cb):
    return lax.dot_general(a, b, (((ca,), (cb,)), ((), ())), preferred_element_type=F32)


def tile_body(l_ref, r_ref, d_ref, w_ref, wt_ref, b_ref, p_ref, gw_ref, gb_ref, gr_ref, gl_ref, o_s, g_s, acc):
    k = pl.program_id(0)
    nj = d_ref.shape[0] // IB
    scale = 1.0 / l_ref.shape[0]
    for eb in range(CL // EB):
        t = dot(l_ref[...], r_ref[:, eb * EB * nj : (eb + 1) * EB * nj], 0, 0)
        t = (t * scale).astype(BF)
        for e1 in range(EB):
            e = eb * EB + e1
            for i in range(IB):
                o_s[e * CL : (e + 1) * CL, i * nj : (i + 1) * nj] = t[
                    i * CL : (i + 1) * CL, e1 * nj : (e1 + 1) * nj
                ]
    for q in range(IB // 2):
        t = dot(w_ref[...], d_ref[q * 2 * nj : (q + 1) * 2 * nj, :], 1, 1).astype(BF)
        for i2 in range(2):
            i = q * 2 + i2
            for e in range(CL):
                g_s[i * CL : (i + 1) * CL, e * nj : (e + 1) * nj] = t[
                    e * CL : (e + 1) * CL, i2 * nj : (i2 + 1) * nj
                ]
    p_ref[...] = (dot(wt_ref[...], o_s[...], 1, 0).T + b_ref[...]).astype(BF)
    gw = dot(o_s[...], d_ref[...], 1, 0)
    gb = jnp.sum(d_ref[...].astype(F32).reshape(-1, 8, CP), axis=0)
    gl_ref[...] = (dot(g_s[...], r_ref[...], 1, 1) * scale).T.astype(BF)
    gr = dot(l_ref[...], g_s[...], 1, 0)

    @pl.when(k == 0)
    def _():
        gw_ref[...] = gw
        gb_ref[...] = gb
        acc[...] = gr

    @pl.when(k != 0)
    def _():
        gw_ref[...] += gw
        gb_ref[...] += gb
        acc[...] += gr

    @pl.when(k == pl.num_programs(0) - 1)
    def _():
        gr_ref[...] = (acc[...] * scale).astype(BF)


def tile(left, right, dpair, w, wt, bias):
    seqs, nj = right.shape[0], right.shape[1] // CL
    n = left.shape[1] // (IB * CL)
    whole = lambda *shape: pl.BlockSpec(shape, lambda k: (0,) * len(shape))
    return pl.pallas_call(
        tile_body,
        grid=(n,),
        out_shape=(
            jax.ShapeDtypeStruct((n * IB * nj, CP), BF),
            jax.ShapeDtypeStruct((CL * CL, CP), F32),
            jax.ShapeDtypeStruct((8, CP), F32),
            jax.ShapeDtypeStruct((seqs, CL * nj), BF),
            jax.ShapeDtypeStruct((seqs, n * IB * CL), BF),
        ),
        in_specs=[
            pl.BlockSpec((seqs, IB * CL), lambda k: (0, k)),
            whole(seqs, CL * nj),
            pl.BlockSpec((IB * nj, CP), lambda k: (k, 0)),
            whole(CL * CL, CP),
            whole(CP, CL * CL),
            whole(1, CP),
        ],
        out_specs=(
            pl.BlockSpec((IB * nj, CP), lambda k: (k, 0)),
            whole(CL * CL, CP),
            whole(8, CP),
            whole(seqs, CL * nj),
            pl.BlockSpec((seqs, IB * CL), lambda k: (0, k)),
        ),
        scratch_shapes=[
            pltpu.VMEM((CL * CL, IB * nj), BF),
            pltpu.VMEM((IB * CL, CL * nj), BF),
            pltpu.VMEM((seqs, CL * nj), F32),
        ],
        compiler_params=pltpu.CompilerParams(
            dimension_semantics=("arbitrary",), vmem_limit_bytes=40 << 20
        ),
        name="tile",
    )(left, right, dpair, w, wt, bias)


def shards(left, right, weight, bias, cotangent):
    nrow, ncol = lax.axis_size("row"), lax.axis_size("col")
    srow, scol = right.shape[0], left.shape[0]
    seqs = srow * nrow
    ni, nj = cotangent.shape[0], cotangent.shape[1]

    def gather(x, axis, n):
        y = jnp.broadcast_to(x[None], (n,) + x.shape)
        return lax.all_to_all(y, axis, 0, 0, tiled=True).reshape(seqs, x.shape[1])

    right_ej = right.reshape(srow, nj, CL).transpose(0, 2, 1).reshape(srow, CL * nj)
    left_full = gather(left, "col", ncol)
    right_full = gather(right_ej, "row", nrow)
    w = weight.reshape(CL, CL, CP).transpose(1, 0, 2).reshape(CL * CL, CP)
    pair, gw, gb, gr, gl = tile(
        left_full, right_full, cotangent.reshape(ni * nj, CP), w, w.T, bias.reshape(1, CP)
    )

    def scatter(x, axis, n):
        y = lax.all_to_all(x.reshape(n, seqs // n, x.shape[1]), axis, 0, 0, tiled=True)
        return jnp.sum(y.astype(F32), axis=0).astype(BF)

    ndev = nrow * ncol
    rows = CL * CL // ndev
    gb = jnp.sum(gb, axis=0)
    tail = jnp.broadcast_to(gb, (ndev, 1, CP))
    both = jnp.concatenate([gw.reshape(ndev, rows, CP), tail], axis=1)
    both = jnp.sum(lax.all_to_all(both, ("row", "col"), 0, 0, tiled=True), axis=0)
    grad_left = scatter(gl, "col", ncol)
    grad_right = scatter(gr, "row", nrow).reshape(srow, CL, nj).transpose(0, 2, 1)
    part = jnp.broadcast_to(both[None, :rows], (ndev, rows, CP))
    gw = lax.all_to_all(part, ("row", "col"), 0, 0, tiled=True)
    gw = gw.reshape(CL, CL, CP).transpose(1, 0, 2).reshape(CL * CL, CP)
    return (
        pair.reshape(ni, nj, CP),
        grad_left,
        grad_right.reshape(srow, nj * CL),
        gw,
        both[rows],
    )


def solution(mesh):
    placed = (P("col", "row"), P("row", "col"), P(), P(), P("row", "col", None))
    return jax.shard_map(
        shards,
        mesh=mesh,
        in_specs=placed,
        out_specs=(P("row", "col", None), P("col", "row"), P("row", "col"), P(), P()),
        check_vma=False,
    )
```

time: 565 us -> 155 us (0.27)
  waiting for transfers between devices: 215 us -> 64.2 us
  matrix products: 119 us -> 0 us
  local copies, waits for them, and re-layouts: 106 us -> 9.46 us
  blocking collectives: 89.9 us -> 23.9 us
  Pallas kernels: 0 us -> 28.1 us
  starting transfers between devices: 0.16 us -> 26.9 us
  between operations: 13.8 us -> 0.72 us
  loops' own time: 11.1 us -> 0 us
  other arithmetic: 8.94 us -> 1.1 us
    psum x1 -> x0, waiting for transfers between devices: 150 us -> none  [shards(): lax.psum((grad_w.reshape(CL * CL, CP), grad_b), ('row', 'col'))]
    dot_general x48 -> x0, matrix products: 119 us -> none  [the longest x8 54.2 us: step(): lax.dot_general(outer, dpair, (((0, 2), (0, 1)), ((), ())), preferred_ele...]
    psum x1 -> x0, blocking collectives: 64.8 us -> none  [shards(): lax.psum((grad_w.reshape(CL * CL, CP), grad_b), ('row', 'col'))]
    all_to_all x0 -> x5, waiting for transfers between devices: none -> 64.2 us  [the longest x2 27 us: scatter(): lax.all_to_all(x.reshape(n, seqs // n, x.shape[1]), axis, 0, 0, tiled=True)]
    reshape x8 -> x3, local copies, waits for them, and re-layouts: 64.4 us -> 2.17 us  [the longest x1 1.11 us: shards(): right.reshape(srow, nj, CL).transpose(0, 2, 1).reshape(srow, CL * nj)]
    unnamed x6 -> x0, waiting for transfers between devices: 38.9 us -> none
    pallas_call x0 -> x1, Pallas kernels: none -> 28.1 us  [tile(): pl.pallas_call(tile_body, grid=(n,), out_shape=(jax.ShapeDtypeStruct((n *...]
    all_to_all x0 -> x5, starting transfers between devices: none -> 26.9 us  [the longest x2 14.5 us: gather(): return lax.all_to_all(y, axis, 0, 0, tiled=True).reshape(seqs, x.shape[1])]
  transfers between devices with their start and end apart: 4 -> 5, of which waited for: 3 -> 5; matrix products, arithmetic and copies ran while one was open for 2% -> 3% of each run, Pallas kernels for 0% -> 0%
where the time goes in v1:
time: 155 us; the launch traced here: 154 us
  waiting for transfers between devices  64.2 us (41%)
  Pallas kernels  28.1 us (18%)
  starting transfers between devices  26.9 us (17%)
  blocking collectives  23.9 us (15%)
  local copies, waits for them, and re-layouts  9.46 us (6%)
    pallas_call x1, Pallas kernels, tile(): pl.pallas_call(tile_body, grid=(n,), out_shape=(jax.ShapeDtypeStruct((n *...  28.1 us
    all_to_all x2, waiting for transfers between devices, scatter(): lax.all_to_all(x.reshape(n, seqs // n, x.shape[1]), axis, 0, 0, tiled=True)  27 us
    all_to_all x2, waiting for transfers between devices, gather(): return lax.all_to_all(y, axis, 0, 0, tiled=True).reshape(seqs, x.shape[1])  25.6 us
    all_to_all x1, blocking collectives, shards(): lax.all_to_all(both, ('row', 'col'), 0, 0, tiled=True)  23.9 us
    all_to_all x2, starting transfers between devices, gather(): return lax.all_to_all(y, axis, 0, 0, tiled=True).reshape(seqs, x.shape[1])  14.5 us
    all_to_all x1, waiting for transfers between devices, shards(): gw = lax.all_to_all(part, ('row', 'col'), 0, 0, tiled=True)  11.6 us
    all_to_all x2, starting transfers between devices, scatter(): lax.all_to_all(x.reshape(n, seqs // n, x.shape[1]), axis, 0, 0, tiled=True)  7.95 us
    all_to_all x1, starting transfers between devices, shards(): gw = lax.all_to_all(part, ('row', 'col'), 0, 0, tiled=True)  4.47 us
  transfers between devices with their start and end apart: 5, of which 5 were waited for; matrix products, arithmetic and copies ran while one was open for 3% of the time, Pallas kernels for 0%

profile of v1, /device:TPU:1, one launch (start us, length us, event | category | flops | bytes accessed | tf_op | source)
XLA Modules:
  0.0 154.4 jit_solution(2418033715894809879)
XLA Ops:
  0.6 1.7 %broadcast_in_dim.10 = bf16[8,16,2048]{2,1,0:T(8,128)(2,1)} broadcast(bf16[16,2048]{1,0:T(8,128)(2,1)} %param.5), dimensions={1,2} | broadcast | bytes 589824 | tf_op jit(solution)/shard_map/broadcast_in_dim | solution.py:112
  2.3 6.4 %all-to-all-start = ((bf16[8,16,2048]{2,1,0:T(8,128)(2,1)}), bf16[8,16,2048]{2,1,0:T(8,128)(2,1)S(1)}, u32[]{:S(2)}, u32[]{:S(2)}) async-start(bf16[8,16,2048]{2,1,0:T(8,128)(2,1)} %broadcast_in_dim.10), calls=%async_computation | async-start | bytes 1048576 | tf_op jit(solution)/shard_map/all_to_all | solution.py:113
  8.7 0.0 copy-start.2
  8.7 1.1 reshape.59
  9.8 0.1 copy.15
  10.0 9.0 %all-to-all-done = bf16[8,16,2048]{2,1,0:T(8,128)(2,1)S(1)} async-done(((bf16[8,16,2048]{2,1,0:T(8,128)(2,1)}), bf16[8,16,2048]{2,1,0:T(8,128)(2,1)S(1)}, u32[]{:S(2)}, u32[]{:S(2)}) %all-to-all-start) | async-done | bytes 524320 | tf_op jit(solution)/shard_map/all_to_all | solution.py:113
  18.9 0.0 copy-start.1
  18.9 1.1 broadcast_in_dim.24
  20.0 8.1 %all-to-all-start.1 = ((bf16[16,8,4096]{2,1,0:T(8,128)(2,1)}), bf16[16,8,4096]{2,1,0:T(8,128)(2,1)S(1)}, u32[]{:S(2)}, u32[]{:S(2)}) async-start(bf16[16,8,4096]{2,1,0:T(8,128)(2,1)} %broadcast_in_dim.24), calls=%async_computation.1 | async-start | bytes 2097152 | tf_op jit(solution)/shard_map/all_to_all | solution.py:113
  28.1 0.0 copy-done.2
  28.1 0.1 copy.16
  28.2 0.1 copy.17
  28.4 16.7 %all-to-all-done.1 = bf16[16,8,4096]{2,1,0:T(8,128)(2,1)S(1)} async-done(((bf16[16,8,4096]{2,1,0:T(8,128)(2,1)}), bf16[16,8,4096]{2,1,0:T(8,128)(2,1)S(1)}, u32[]{:S(2)}, u32[]{:S(2)}) %all-to-all-start.1) | async-done | bytes 1048608 | tf_op jit(solution)/shard_map/all_to_all | solution.py:113
  45.1 0.0 copy-done.1
  45.1 1.6 %copy-done = bf16[64,128,128]{2,1,0:T(8,128)(2,1)S(1)} copy-done((bf16[64,128,128]{2,1,0:T(8,128)(2,1)S(1)}, bf16[64,128,128]{2,1,0:T(8,128)(2,1)}, u32[]{:S(2)}) %copy-start) | copy-done | bytes 2097176
  46.7 28.1 %tile.1 = (bf16[8192,128]{1,0:T(8,128)(2,1)}, f32[1024,128]{1,0:T(8,128)S(1)}, f32[8,128]{1,0:T(8,128)S(1)}, bf16[128,4096]{1,0:T(8,128)(2,1)}, bf16[128,2048]{1,0:T(8,128)(2,1)}) custom-call(bf16[128,2048]{1,0:T(8,128)(2,1)S(1)} %bitcast.34, bf16[128,4096]{1,0:T(8,128)(2,1)S(1)} %bitcast.31, bf16[8192,128]{1,0:T(8,128)(2,1)S(1)} %bitcast.35, ...), custom_call_target="tpu_custom_call" | custom-call | tf_op jit(solution)/shard_map/tile/pallas_call | solution.py:68
  74.8 3.5 %all-to-all-start.2 = ((bf16[8,16,2048]{2,1,0:T(8,128)(2,1)}), bf16[8,16,2048]{2,1,0:T(8,128)(2,1)S(1)}, u32[]{:S(2)}, u32[]{:S(2)}) async-start(bf16[8,16,2048]{2,1,0:T(8,128)(2,1)} %bitcast.10), calls=%async_computation.2 | async-start | bytes 1048576 | tf_op jit(solution)/shard_map/all_to_all | solution.py:124
  78.4 0.1 pad_maximum_fusion
  78.5 10.0 %all-to-all-done.2 = bf16[8,16,2048]{2,1,0:T(8,128)(2,1)S(1)} async-done(((bf16[8,16,2048]{2,1,0:T(8,128)(2,1)}), bf16[8,16,2048]{2,1,0:T(8,128)(2,1)S(1)}, u32[]{:S(2)}, u32[]{:S(2)}) %all-to-all-start.2) | async-done | bytes 524320 | tf_op jit(solution)/shard_map/all_to_all | solution.py:124
  88.5 23.9 %all_to_all.30 = f32[128,9,128]{2,1,0:T(8,128)S(1)} all-to-all(f32[128,9,128]{2,1,0:T(8,128)S(1)} %pad_maximum_fusion), channel_id=1, replica_groups=mesh['row'=16,'col'=8] {'row','col'}, dimensions={0} | all-to-all | bytes 1179648 | tf_op jit(solution)/shard_map/all_to_all | solution.py:132
  112.3 4.5 %all-to-all-start.3 = ((bf16[16,8,4096]{2,1,0:T(8,128)(2,1)}), bf16[16,8,4096]{2,1,0:T(8,128)(2,1)S(1)}, u32[]{:S(2)}, u32[]{:S(2)}) async-start(bf16[16,8,4096]{2,1,0:T(8,128)(2,1)} %bitcast.11), calls=%async_computation.3 | async-start | bytes 2097152 | tf_op jit(solution)/shard_map/all_to_all | solution.py:124
  116.8 0.1 reduce_sum.45
  117.0 16.9 %all-to-all-done.3 = bf16[16,8,4096]{2,1,0:T(8,128)(2,1)S(1)} async-done(((bf16[16,8,4096]{2,1,0:T(8,128)(2,1)}), bf16[16,8,4096]{2,1,0:T(8,128)(2,1)S(1)}, u32[]{:S(2)}, u32[]{:S(2)}) %all-to-all-start.3) | async-done | bytes 1048608 | tf_op jit(solution)/shard_map/all_to_all | solution.py:124
  133.9 0.8 broadcast_in_dim.26
  134.7 4.5 %all-to-all-start.5 = ((f32[128,8,128]{2,1,0:T(8,128)}), f32[128,8,128]{2,1,0:T(8,128)S(1)}, u32[]{:S(2)}, u32[]{:S(2)}) async-start(f32[128,8,128]{2,1,0:T(8,128)} %broadcast_in_dim.26), calls=%async_computation.5 | async-start | bytes 1048576 | tf_op jit(solution)/shard_map/all_to_all | solution.py:136
  139.2 0.7 reduce_sum.42
  139.9 0.5 slice_bitcast_fusion
  140.4 0.1 reduce_sum.43
  140.6 0.2 copy.18
  140.8 0.9 reshape.69
  141.7 11.6 %all-to-all-done.5 = f32[128,8,128]{2,1,0:T(8,128)S(1)} async-done(((f32[128,8,128]{2,1,0:T(8,128)}), f32[128,8,128]{2,1,0:T(8,128)S(1)}, u32[]{:S(2)}, u32[]{:S(2)}) %all-to-all-start.5) | async-done | bytes 524320 | tf_op jit(solution)/shard_map/all_to_all | solution.py:136
  153.3 1.1 copy.19
  (6 shorter events, 0.1 us)
Async XLA Ops:
  2.3 16.6 %all-to-all-start = ((bf16[8,16,2048]{2,1,0:T(8,128)(2,1)}), bf16[8,16,2048]{2,1,0:T(8,128)(2,1)S(1)}, u32[]{:S(2)}, u32[]{:S(2)}) async-start(bf16[8,16,2048]{2,1,0:T(8,128)(2,1)} %broadcast_in_dim.10), calls=%async_computation | async-start | bytes 1048576 | tf_op jit(solution)/shard_map/all_to_all | solution.py:113
  8.7 19.4 %copy-start.2 = (bf16[1024,128]{1,0:T(8,128)(2,1)S(1)}, bf16[1024,128]{1,0:T(8,128)(2,1)}, u32[]{:S(2)}) copy-start(bf16[1024,128]{1,0:T(8,128)(2,1)} %param.7) | copy-start | bytes 786436
  18.9 26.1 %copy-start.1 = (f32[128]{0:T(128)S(1)}, f32[128]{0:T(128)}, u32[]{:S(2)}) copy-start(f32[128]{0:T(128)} %param.8) | copy-start | bytes 1540
  20.0 25.1 %all-to-all-start.1 = ((bf16[16,8,4096]{2,1,0:T(8,128)(2,1)}), bf16[16,8,4096]{2,1,0:T(8,128)(2,1)S(1)}, u32[]{:S(2)}, u32[]{:S(2)}) async-start(bf16[16,8,4096]{2,1,0:T(8,128)(2,1)} %broadcast_in_dim.24), calls=%async_computation.1 | async-start | bytes 2097152 | tf_op jit(solution)/shard_map/all_to_all | solution.py:113
  45.1 1.6 %copy-start = (bf16[64,128,128]{2,1,0:T(8,128)(2,1)S(1)}, bf16[64,128,128]{2,1,0:T(8,128)(2,1)}, u32[]{:S(2)}) copy-start(bf16[64,128,128]{2,1,0:T(8,128)(2,1)} %param.9) | copy-start | bytes 6291460
  74.8 13.7 %all-to-all-start.2 = ((bf16[8,16,2048]{2,1,0:T(8,128)(2,1)}), bf16[8,16,2048]{2,1,0:T(8,128)(2,1)S(1)}, u32[]{:S(2)}, u32[]{:S(2)}) async-start(bf16[8,16,2048]{2,1,0:T(8,128)(2,1)} %bitcast.10), calls=%async_computation.2 | async-start | bytes 1048576 | tf_op jit(solution)/shard_map/all_to_all | solution.py:124
  112.3 21.5 %all-to-all-start.3 = ((bf16[16,8,4096]{2,1,0:T(8,128)(2,1)}), bf16[16,8,4096]{2,1,0:T(8,128)(2,1)S(1)}, u32[]{:S(2)}, u32[]{:S(2)}) async-start(bf16[16,8,4096]{2,1,0:T(8,128)(2,1)} %bitcast.11), calls=%async_computation.3 | async-start | bytes 2097152 | tf_op jit(solution)/shard_map/all_to_all | solution.py:124
  134.7 18.6 %all-to-all-start.5 = ((f32[128,8,128]{2,1,0:T(8,128)}), f32[128,8,128]{2,1,0:T(8,128)S(1)}, u32[]{:S(2)}, u32[]{:S(2)}) async-start(f32[128,8,128]{2,1,0:T(8,128)} %broadcast_in_dim.26), calls=%async_computation.5 | async-start | bytes 1048576 | tf_op jit(solution)/shard_map/all_to_all | solution.py:136

commit v2 on v1

v2 whole, which is shorter than its diff:
```python
import jax
import jax.numpy as jnp
from jax import lax
from jax.experimental import pallas as pl
from jax.experimental.pallas import tpu as pltpu
from jax.sharding import PartitionSpec as P


CL = 32
CP = 128
FB = 16
IB = 8
EB = 8
BF = jnp.bfloat16
F32 = jnp.float32

NX, NZ, NC, NY = 4, 2, 2, 4


def row_shift(dx, dz, dc):
    place = lambda x, z, c: (x * NZ + z) * NC + c
    return [
        (place(x, z, c), place((x + dx) % NX, (z + dz) % NZ, (c + dc) % NC))
        for x in range(NX)
        for z in range(NZ)
        for c in range(NC)
    ]


def col_shift(dz, dy):
    return [(z * NY + y, (z + dz) % NZ * NY + (y + dy) % NY) for z in range(NZ) for y in range(NY)]


def dot(a, b, ca, cb):
    return lax.dot_general(a, b, (((ca,), (cb,)), ((), ())), preferred_element_type=F32)


def whole(*shape):
    return pl.BlockSpec(shape, lambda k: (0,) * len(shape))


def left_block(pieces, l_s):
    col = lax.axis_index("col")
    z, y = col // NY, col % NY
    for d in range(NY):
        for b in range(NZ):
            l_s[(z + b) % NZ * NY + (y + NY - d) % NY] = pieces[d][b]
    return l_s[...].reshape(l_s.shape[0] * l_s.shape[1], l_s.shape[2])


def forward_body(l0, l1, l2, l3, r_ref, d_ref, wt_ref, b_ref, p_ref, gw_ref, gb_ref, rt_ref, l_s):
    k = pl.program_id(0)
    nj = d_ref.shape[0] // FB
    left = left_block((l0, l1, l2, l3), l_s).T
    scale = 1.0 / left.shape[1]
    part = rt_ref.shape[0]
    rt_ref[...] = r_ref[:, pl.ds(pl.multiple_of(k * part, part), part)].T
    rows = []
    for eb in range(CL // EB):
        t = dot(left, r_ref[:, eb * EB * nj : (eb + 1) * EB * nj], 1, 0)
        t = (t * scale).astype(BF)
        for e1 in range(EB):
            rows.append(
                jnp.concatenate(
                    [t[i * CL : (i + 1) * CL, e1 * nj : (e1 + 1) * nj] for i in range(FB)], axis=1
                )
            )
    outer = jnp.concatenate(rows, axis=0)
    p_ref[...] = (dot(wt_ref[...], outer, 1, 0).T + b_ref[...]).astype(BF)
    gw = dot(outer, d_ref[...], 1, 0)
    gb = jnp.sum(d_ref[...].astype(F32).reshape(-1, 8, CP), axis=0)

    @pl.when(k == 0)
    def _():
        gw_ref[...] = gw
        gb_ref[...] = gb

    @pl.when(k != 0)
    def _():
        gw_ref[...] += gw
        gb_ref[...] += gb


def backward_body(
    l0, l1, l2, l3, rt_ref, d_ref, w_ref, g0, g1, g2, g3, keep_ref, send_ref, l_s, gl_s, acc
):
    k = pl.program_id(0)
    nj = d_ref.shape[0] // IB
    left = left_block((l0, l1, l2, l3), l_s)
    scale = 1.0 / left.shape[0]
    rows = []
    for q in range(IB // 2):
        t = dot(w_ref[...], d_ref[q * 2 * nj : (q + 1) * 2 * nj, :], 1, 1).astype(BF)
        for i2 in range(2):
            rows.append(
                jnp.concatenate(
                    [t[e * CL : (e + 1) * CL, i2 * nj : (i2 + 1) * nj] for e in range(CL)], axis=1
                )
            )
    grad = jnp.concatenate(rows, axis=0)
    gl_s[...] = (dot(grad, rt_ref[...], 1, 0) * scale).T.reshape(gl_s.shape)
    col = lax.axis_index("col")
    z, y = col // NY, col % NY
    for d, out in enumerate((g0, g1, g2, g3)):
        for b in range(NZ):
            out[b] = gl_s[(z + b) % NZ * NY + (y + d) % NY].astype(out.dtype)
    gr = dot(left, grad, 1, 0).reshape(acc.shape)

    @pl.when(k == 0)
    def _():
        acc[...] = gr

    @pl.when(k != 0)
    def _():
        acc[...] += gr

    @pl.when(k == pl.num_programs(0) - 1)
    def _():
        row = lax.axis_index("row")
        x, zh, core = row // (NZ * NC), row // NC % NZ, row % NC
        for dx in range(NX):
            for b in range(NZ):
                at = ((x + dx) % NX * NZ + (zh + b) % NZ) * NC
                keep_ref[dx * NZ + b] = acc[at + core] * scale
                send_ref[dx * NZ + b] = (acc[at + 1 - core] * scale).astype(BF)


def params(mib):
    return pltpu.CompilerParams(dimension_semantics=("arbitrary",), vmem_limit_bytes=mib << 20)


def forward(pieces, right, dpair, wt, bias):
    scol, width = pieces[0].shape[1:]
    seqs, nj = right.shape[0], right.shape[1] // CL
    n = width // (FB * CL)
    return pl.pallas_call(
        forward_body,
        grid=(n,),
        out_shape=(
            jax.ShapeDtypeStruct((n * FB * nj, CP), BF),
            pltpu.HBM((CL * CL, CP), F32),
            jax.ShapeDtypeStruct((8, CP), F32),
            pltpu.HBM((CL * nj, seqs), BF),
        ),
        in_specs=[pl.BlockSpec((NZ, scol, FB * CL), lambda k: (0, 0, k))] * NY
        + [
            whole(seqs, CL * nj),
            pl.BlockSpec((FB * nj, CP), lambda k: (k, 0)),
            whole(CP, CL * CL),
            whole(1, CP),
        ],
        out_specs=(
            pl.BlockSpec((FB * nj, CP), lambda k: (k, 0)),
            whole(CL * CL, CP),
            whole(8, CP),
            pl.BlockSpec((CL * nj // n, seqs), lambda k: (k, 0)),
        ),
        scratch_shapes=[pltpu.VMEM((NZ * NY, scol, FB * CL), BF)],
        compiler_params=params(40),
        name="forward",
    )(*pieces, right, dpair, wt, bias)


def backward(pieces, right_t, dpair, w):
    scol, width = pieces[0].shape[1:]
    seqs, nj = right_t.shape[1], right_t.shape[0] // CL
    n = width // (IB * CL)
    srow = seqs // (NX * NZ * NC)
    gl_spec = pl.BlockSpec((NZ, scol, IB * CL), lambda k: (0, 0, k))
    half = (NX * NZ, srow, CL * nj)
    return pl.pallas_call(
        backward_body,
        grid=(n,),
        out_shape=(
            pltpu.HBM((NZ, scol, width), F32),
            pltpu.HBM((NZ, scol, width), BF),
            pltpu.HBM((NZ, scol, width), BF),
            pltpu.HBM((NZ, scol, width), BF),
            pltpu.HBM(half, F32),
            pltpu.HBM(half, BF),
        ),
        in_specs=[pl.BlockSpec((NZ, scol, IB * CL), lambda k: (0, 0, k))] * NY
        + [
            whole(CL * nj, seqs),
            pl.BlockSpec((IB * nj, CP), lambda k: (k, 0)),
            whole(CL * CL, CP),
        ],
        out_specs=(gl_spec,) * NY + (whole(*half),) * 2,
        scratch_shapes=[
            pltpu.VMEM((NZ * NY, scol, IB * CL), BF),
            pltpu.VMEM((NZ * NY, scol, IB * CL), F32),
            pltpu.VMEM((NX * NZ * NC, srow, CL * nj), F32),
        ],
        compiler_params=params(24),
        name="backward",
    )(*pieces, right_t, dpair, w)


def shards(left, right, weight, bias, cotangent):
    ndev = lax.axis_size("row") * lax.axis_size("col")
    srow = right.shape[0]
    seqs = srow * lax.axis_size("row")
    ni, nj = cotangent.shape[0], cotangent.shape[1]
    same_core = [[xz * NC + c for xz in range(NX * NZ)] for c in range(NC)]
    core = lax.axis_index("row") & 1

    other = lax.ppermute(left, "col", col_shift(1, 0))
    mine = right.reshape(srow, nj, CL).transpose(0, 2, 1).reshape(1, srow, CL * nj)
    mine = jnp.broadcast_to(mine, (NX * NZ, srow, CL * nj))
    mine = lax.all_to_all(mine, "row", 0, 0, tiled=True, axis_index_groups=same_core)
    pair = jnp.stack([left, other])
    pieces = [pair] + [lax.ppermute(pair, "col", col_shift(0, d)) for d in range(1, NY)]
    theirs = lax.ppermute(mine, "row", row_shift(0, 0, 1))
    first = jnp.where(core == 0, mine, theirs)
    second = jnp.where(core == 0, theirs, mine)
    right_full = jnp.stack([first, second], axis=1).reshape(seqs, CL * nj)

    dpair = cotangent.reshape(ni * nj, CP)
    w = weight.reshape(CL, CL, CP).transpose(1, 0, 2).reshape(CL * CL, CP)
    pair_update, gw, gb, right_t = forward(pieces, right_full, dpair, w.T, bias.reshape(1, CP))

    rows = CL * CL // ndev
    gw, dpair = lax.optimization_barrier((gw, dpair))
    gw = lax.all_to_all(gw.reshape(ndev, rows, CP), ("row", "col"), 0, 0, tiled=True)
    gw = jnp.concatenate([jnp.sum(gw, axis=0), jnp.sum(gb, axis=0, keepdims=True)], axis=0)

    l0, l1, l2, l3, keep, send = backward(pieces, right_t, dpair, w)

    gw = jnp.broadcast_to(gw.reshape(1, 1, (rows + 1) * CP), (ndev, 1, (rows + 1) * CP))
    gw = lax.all_to_all(gw, ("row", "col"), 0, 0, tiled=True)
    grad_b = jnp.sum(gw[:, 0, rows * CP :], axis=0)
    grad_w = gw[:, 0, : rows * CP].reshape(CL, CL, CP).transpose(1, 0, 2).reshape(CL * CL, CP)

    got = lax.ppermute(send, "row", row_shift(0, 0, 1))
    part = [keep[NZ * d : NZ * (d + 1)] + got[NZ * d : NZ * (d + 1)].astype(F32) for d in range(NX)]
    away = [p.astype(BF) for p in part[1:]]
    rgot = [lax.ppermute(p, "row", row_shift(d + 1, 0, 0)) for d, p in enumerate(away)]
    lgot = [lax.ppermute(g, "col", col_shift(0, d)) for d, g in ((1, l1), (2, l2), (3, l3))]
    lsum = l0 + sum(g.astype(F32) for g in lgot)
    lfar = lsum[1].astype(BF)
    lz = lax.ppermute(lfar, "col", col_shift(1, 0))
    rsum = part[0] + sum(g.astype(F32) for g in rgot)
    rfar = rsum[1].astype(BF)
    rz = lax.ppermute(rfar, "row", row_shift(0, 1, 0))
    grad_left = (lsum[0] + lz.astype(F32)).astype(BF)
    grad_right = (rsum[0] + rz.astype(F32)).astype(BF)
    grad_right = grad_right.reshape(srow, CL, nj).transpose(0, 2, 1).reshape(srow, nj * CL)
    return (pair_update.reshape(ni, nj, CP), grad_left, grad_right, grad_w, grad_b)


def solution(mesh):
    placed = (P("col", "row"), P("row", "col"), P(), P(), P("row", "col", None))
    return jax.shard_map(
        shards,
        mesh=mesh,
        in_specs=placed,
        out_specs=(P("row", "col", None), P("col", "row"), P("row", "col"), P(), P()),
        check_vma=False,
    )
```

time: 155 us -> 115 us (0.74)
  waiting for transfers between devices: 64.2 us -> 27.7 us
  blocking collectives: 23.9 us -> 17.7 us
  local copies, waits for them, and re-layouts: 9.46 us -> 6.18 us
  starting transfers between devices: 26.9 us -> 30.1 us
  other arithmetic: 1.1 us -> 2.83 us
    all_to_all x5 -> x2, waiting for transfers between devices: 64.2 us -> 12.6 us  [the longest x1 7.36 us: shards(): lax.all_to_all(gw.reshape(ndev, rows, CP), ('row', 'col'), 0, 0, tiled=True)]
    ppermute x0 -> x14, starting transfers between devices: none -> 20.4 us  [the longest x3 4.39 us: shards(): lax.ppermute(p, 'row', row_shift(d + 1, 0, 0))]
    all_to_all x5 -> x2, starting transfers between devices: 26.9 us -> 9.72 us  [the longest x1 5.3 us: shards(): lax.all_to_all(gw.reshape(ndev, rows, CP), ('row', 'col'), 0, 0, tiled=True)]
    ppermute x0 -> x14, waiting for transfers between devices: none -> 15.1 us  [the longest x3 8.23 us: shards(): lax.ppermute(pair, 'col', col_shift(0, d))]
    all_to_all x1, blocking collectives: 23.9 us -> 17.7 us  [shards(): lax.all_to_all(mine, 'row', 0, 0, tiled=True, axis_index_groups=same_core)]
    broadcast_in_dim x4 -> x2, local copies, waits for them, and re-layouts: 3.62 us -> 1.16 us  [the longest x1 1.13 us: shards(): jnp.broadcast_to(gw.reshape(1, 1, (rows + 1) * CP), (ndev, 1, (rows + 1)...]
    pallas_call x1 -> x2, Pallas kernels: 28.1 us -> 29.1 us  [the longest x1 15.8 us: backward(): pl.pallas_call(backward_body, grid=(n,), out_shape=(pltpu.HBM((NZ, scol,...]
  transfers between devices with their start and end apart: 5 -> 16, of which waited for: 5 -> 7; matrix products, arithmetic and copies ran while one was open for 3% -> 4% of each run, Pallas kernels for 0% -> 0%
where the time goes in v2:
time: 115 us; the launch traced here: 114 us
  starting transfers between devices  30.1 us (26%)
  Pallas kernels  29.1 us (25%)
  waiting for transfers between devices  27.7 us (24%)
  blocking collectives  17.7 us (15%)
  local copies, waits for them, and re-layouts  6.18 us (5%)
  other arithmetic  2.83 us (2%)
    all_to_all x1, blocking collectives, shards(): lax.all_to_all(mine, 'row', 0, 0, tiled=True, axis_index_groups=same_core)  17.7 us
    pallas_call x1, Pallas kernels, backward(): pl.pallas_call(backward_body, grid=(n,), out_shape=(pltpu.HBM((NZ, scol,...  15.8 us
    pallas_call x1, Pallas kernels, forward(): pl.pallas_call(forward_body, grid=(n,), out_shape=(jax.ShapeDtypeStruct((...  13.2 us
    ppermute x3, waiting for transfers between devices, shards(): lax.ppermute(pair, 'col', col_shift(0, d))  8.23 us
    all_to_all x1, waiting for transfers between devices, shards(): lax.all_to_all(gw.reshape(ndev, rows, CP), ('row', 'col'), 0, 0, tiled=True)  7.36 us
    all_to_all x1, starting transfers between devices, shards(): lax.all_to_all(gw.reshape(ndev, rows, CP), ('row', 'col'), 0, 0, tiled=True)  5.3 us
    all_to_all x1, waiting for transfers between devices, shards(): gw = lax.all_to_all(gw, ('row', 'col'), 0, 0, tiled=True)  5.21 us
    all_to_all x1, starting transfers between devices, shards(): gw = lax.all_to_all(gw, ('row', 'col'), 0, 0, tiled=True)  4.43 us
  transfers between devices with their start and end apart: 16, of which 7 were waited for; matrix products, arithmetic and copies ran while one was open for 4% of the time, Pallas kernels for 0%

profile of v2, /device:TPU:1, one launch (start us, length us, event | category | flops | bytes accessed | tf_op | source)
XLA Modules:
  0.0 114.4 jit_solution(18326953931988473484)
XLA Ops:
  0.7 1.1 reshape.51
  2.0 17.7 %all_to_all.15 = bf16[8,8,4096]{2,1,0:T(8,128)(2,1)S(1)} all-to-all(bf16[8,8,4096]{2,1,0:T(8,128)(2,1)S(1)} %broadcast_in_dim.18), channel_id=1, replica_groups={{0,16,32,48,64,80,96,112},{8,24,40,56,72,88,104,120},{1,17,33,49,65,81,..., dimensions={0} | all-to-all | bytes 1048576 | tf_op jit(solution)/shard_map/all_to_all | solution.py:210
  19.7 2.4 %collective-permute-start.4 = (bf16[8,8,4096]{2,1,0:T(8,128)(2,1)S(1)}, bf16[8,8,4096]{2,1,0:T(8,128)(2,1)S(1)}, u32[]{:S(2)}, u32[]{:S(2)}) collective-permute-start(bf16[8,8,4096]{2,1,0:T(8,128)(2,1)S(1)} %all_to_all.15), channel_id=1, source_target_pairs={{0,8},{8,0},{16,24},{24,16},{32,40},{40,32},{48,56},{56,48},{64,72... | collective-permute-start | bytes 1572872 | tf_op jit(solution)/shard_map/ppermute | solution.py:213
  22.1 0.7 collective-permute-start
  23.1 2.6 %collective-permute-done = bf16[16,2048]{1,0:T(8,128)(2,1)S(1)} collective-permute-done((bf16[16,2048]{1,0:T(8,128)(2,1)S(1)}, bf16[16,2048]{1,0:T(8,128)(2,1)S(1)}, u32[]{:S(2)}, u32[]{:S(2)}) %collective-permute-start) | collective-permute-done | bytes 65568 | tf_op jit(solution)/shard_map/ppermute | solution.py:207
  25.8 2.8 %collective-permute-start.3 = (bf16[2,16,2048]{2,1,0:T(8,128)(2,1)S(1)}, bf16[2,16,2048]{2,1,0:T(8,128)(2,1)S(1)}, u32[]{:S(2)}, u32[]{:S(2)}) collective-permute-start(bf16[2,16,2048]{2,1,0:T(8,128)(2,1)S(1)} %pad_maximum_fusion.1.l0), channel_id=1, source_target_pairs={{0,3},{1,0},{2,1},{3,2},{4,7},{5,4},{6,5},{7,6},{8,11},{9,8},{10,9... | collective-permute-start | bytes 393224 | tf_op jit(solution)/shard_map/ppermute | solution.py:212
  28.6 0.3 collective-permute-start.2
  29.0 0.7 collective-permute-start.1
  29.8 3.7 %collective-permute-done.3.l3 = bf16[2,16,2048]{2,1,0:T(8,128)(2,1)S(1)} collective-permute-done((bf16[2,16,2048]{2,1,0:T(8,128)(2,1)S(1)}, bf16[2,16,2048]{2,1,0:T(8,128)(2,1)S(1)}, u32[]{:S(2)}, u32[]{:S(2)}) %collective-permute-start.3) | collective-permute-done | bytes 131104 | tf_op jit(solution)/shard_map/ppermute | solution.py:212
  33.6 0.5 collective-permute-done.2.l2
  34.0 4.0 %collective-permute-done.1.l1 = bf16[2,16,2048]{2,1,0:T(8,128)(2,1)S(1)} collective-permute-done((bf16[2,16,2048]{2,1,0:T(8,128)(2,1)S(1)}, bf16[2,16,2048]{2,1,0:T(8,128)(2,1)S(1)}, u32[]{:S(2)}, u32[]{:S(2)}) %collective-permute-start.1) | collective-permute-done | bytes 131104 | tf_op jit(solution)/shard_map/ppermute | solution.py:212
  38.1 13.2 %forward.1 = (bf16[8192,128]{1,0:T(8,128)(2,1)}, f32[1024,128]{1,0:T(8,128)}, f32[8,128]{1,0:T(8,128)S(1)}, bf16[4096,128]{1,0:T(8,128)(2,1)}) custom-call(bf16[2,16,2048]{2,1,0:T(8,128)(2,1)S(1)} %pad_maximum_fusion.1.l0, bf16[2,16,2048]{2,1,0:T(8,128)(2,1)S(1)} %collective-permute-done.1.l1, bf16[2,16,2048]{2,1,0:T(8,128)(2,1)S(1)} %collective-permute-done.2.l2, ...), custom_call_target="tpu_custom_call" | custom-call | tf_op jit(solution)/shard_map/forward/pallas_call | solution.py:136
  51.3 1.2 %copy-done.1 = bf16[4096,128]{1,0:T(8,128)(2,1)S(1)} copy-done((bf16[4096,128]{1,0:T(8,128)(2,1)S(1)}, bf16[4096,128]{1,0:T(8,128)(2,1)}, u32[]{:S(2)}) %copy-start.1) | copy-done | bytes 1048600
  52.5 15.8 %backward.1 = (f32[2,16,2048]{2,1,0:T(8,128)}, bf16[2,16,2048]{2,1,0:T(8,128)(2,1)}, bf16[2,16,2048]{2,1,0:T(8,128)(2,1)}, bf16[2,16,2048]{2,1,0:T(8,128)(2,1)},...) custom-call(bf16[2,16,2048]{2,1,0:T(8,128)(2,1)S(1)} %pad_maximum_fusion.1.l0, ...), custom_call_target="tpu_custom_call" | custom-call | tf_op jit(solution)/shard_map/backward/pallas_call | solution.py:171
  68.7 2.4 %collective-permute-start.7 = (bf16[2,16,2048]{2,1,0:T(8,128)(2,1)}, bf16[2,16,2048]{2,1,0:T(8,128)(2,1)S(1)}, u32[]{:S(2)}, u32[]{:S(2)}) collective-permute-start(bf16[2,16,2048]{2,1,0:T(8,128)(2,1)} %get-tuple-element.24), channel_id=1, source_target_pairs={{0,3},{1,0},{2,1},{3,2},{4,7},{5,4},{6,5},{7,6},{8,11},{9,8},{10,9... | collective-permute-start | bytes 393224 | tf_op jit(solution)/shard_map/ppermute | solution.py:238
  71.1 1.3 %collective-permute-start.9 = (bf16[8,8,4096]{2,1,0:T(8,128)(2,1)}, bf16[8,8,4096]{2,1,0:T(8,128)(2,1)S(1)}, u32[]{:S(2)}, u32[]{:S(2)}) collective-permute-start(bf16[8,8,4096]{2,1,0:T(8,128)(2,1)} %get-tuple-element.26), channel_id=1, source_target_pairs={{0,8},{8,0},{16,24},{24,16},{32,40},{40,32},{48,56},{56,48},{64,72... | collective-permute-start | bytes 1572872 | tf_op jit(solution)/shard_map/ppermute | solution.py:234
  72.5 5.3 %all-to-all-start.1 = ((f32[128,8,128]{2,1,0:T(8,128)}), f32[128,8,128]{2,1,0:T(8,128)S(1)}, u32[]{:S(2)}, u32[]{:S(2)}) async-start(f32[128,8,128]{2,1,0:T(8,128)} %bitcast.21), calls=%async_computation.1 | async-start | bytes 1048576 | tf_op jit(solution)/shard_map/all_to_all | solution.py:224
  77.8 1.0 add_add_fusion.1
  78.9 1.4 %collective-permute-start.10 = (bf16[2,8,4096]{2,1,0:T(8,128)(2,1)S(1)}, bf16[2,8,4096]{2,1,0:T(8,128)(2,1)S(1)}, u32[]{:S(2)}, u32[]{:S(2)}) collective-permute-start(bf16[2,8,4096]{2,1,0:T(8,128)(2,1)S(1)} %get-tuple-element.29), channel_id=1, source_target_pairs={{0,32},{8,40},{16,48},{24,56},{32,64},{40,72},{48,80},{56,88},{64,... | collective-permute-start | bytes 393224 | tf_op jit(solution)/shard_map/ppermute | solution.py:237
  80.4 1.3 %collective-permute-start.12 = (bf16[2,8,4096]{2,1,0:T(8,128)(2,1)S(1)}, bf16[2,8,4096]{2,1,0:T(8,128)(2,1)S(1)}, u32[]{:S(2)}, u32[]{:S(2)}) collective-permute-start(bf16[2,8,4096]{2,1,0:T(8,128)(2,1)S(1)} %get-tuple-element.30), channel_id=1, source_target_pairs={{0,96},{8,104},{16,112},{24,120},{32,0},{40,8},{48,16},{56,24},{64... | collective-permute-start | bytes 393224 | tf_op jit(solution)/shard_map/ppermute | solution.py:237
  81.7 1.6 %collective-permute-start.11 = (bf16[2,8,4096]{2,1,0:T(8,128)(2,1)S(1)}, bf16[2,8,4096]{2,1,0:T(8,128)(2,1)S(1)}, u32[]{:S(2)}, u32[]{:S(2)}) collective-permute-start(bf16[2,8,4096]{2,1,0:T(8,128)(2,1)S(1)} %get-tuple-element.31), channel_id=1, source_target_pairs={{0,64},{8,72},{16,80},{24,88},{32,96},{40,104},{48,112},{56,120},{... | collective-permute-start | bytes 393224 | tf_op jit(solution)/shard_map/ppermute | solution.py:237
  83.3 1.4 %collective-permute-start.8 = (bf16[16,2048]{1,0:T(8,128)(2,1)S(1)}, bf16[16,2048]{1,0:T(8,128)(2,1)S(1)}, u32[]{:S(2)}, u32[]{:S(2)}) collective-permute-start(bf16[16,2048]{1,0:T(8,128)(2,1)S(1)} %fusion.4), channel_id=1, source_target_pairs={{0,4},{1,5},{2,6},{3,7},{4,0},{5,1},{6,2},{7,3},{8,12},{9,13},{10,... | collective-permute-start | bytes 196616 | tf_op jit(solution)/shard_map/ppermute | solution.py:241
  84.8 7.4 %all-to-all-done.1 = f32[128,8,128]{2,1,0:T(8,128)S(1)} async-done(((f32[128,8,128]{2,1,0:T(8,128)}), f32[128,8,128]{2,1,0:T(8,128)S(1)}, u32[]{:S(2)}, u32[]{:S(2)}) %all-to-all-start.1) | async-done | bytes 524320 | tf_op jit(solution)/shard_map/all_to_all | solution.py:224
  92.3 1.1 broadcast_in_dim.21
  93.4 4.4 %all-to-all-start.2 = ((f32[128,1,1152]{2,1,0:T(1,128)}), f32[128,1,1152]{2,1,0:T(1,128)S(1)}, u32[]{:S(2)}, u32[]{:S(2)}) async-start(f32[128,1,1152]{2,1,0:T(1,128)} %broadcast_in_dim.21), calls=%async_computation.2 | async-start | bytes 1179648 | tf_op jit(solution)/shard_map/all_to_all | solution.py:230
  98.0 3.5 %collective-permute-start.13 = (bf16[8,4096]{1,0:T(8,128)(2,1)S(1)}, bf16[8,4096]{1,0:T(8,128)(2,1)S(1)}, u32[]{:S(2)}, u32[]{:S(2)}) collective-permute-start(bf16[8,4096]{1,0:T(8,128)(2,1)S(1)} %fusion.6), channel_id=1, source_target_pairs={{0,16},{8,24},{16,0},{24,8},{32,48},{40,56},{48,32},{56,40},{64,80... | collective-permute-start | bytes 196616 | tf_op jit(solution)/shard_map/ppermute | solution.py:244
  101.4 0.6 fusion.3
  102.1 4.2 %collective-permute-done.13 = bf16[8,4096]{1,0:T(8,128)(2,1)S(1)} collective-permute-done((bf16[8,4096]{1,0:T(8,128)(2,1)S(1)}, bf16[8,4096]{1,0:T(8,128)(2,1)S(1)}, u32[]{:S(2)}, u32[]{:S(2)}) %collective-permute-start.13) | collective-permute-done | bytes 65568 | tf_op jit(solution)/shard_map/ppermute | solution.py:244
  106.5 0.9 reshape.59
  107.4 5.2 %all-to-all-done.2 = f32[128,1,1152]{2,1,0:T(1,128)S(1)} async-done(((f32[128,1,1152]{2,1,0:T(1,128)}), f32[128,1,1152]{2,1,0:T(1,128)S(1)}, u32[]{:S(2)}, u32[]{:S(2)}) %all-to-all-start.2) | async-done | bytes 589856 | tf_op jit(solution)/shard_map/all_to_all | solution.py:230
  112.7 1.1 copy.30
  113.8 0.7 slice_reduce_fusion
  (40 shorter events, 1.6 us)
Async XLA Ops:
  0.6 21.5 %copy-start.5 = (bf16[16,2048]{1,0:T(8,128)(2,1)S(1)}, bf16[16,2048]{1,0:T(8,128)(2,1)}, u32[]{:S(2)}) copy-start(bf16[16,2048]{1,0:T(8,128)(2,1)} %param.5) | copy-start | bytes 196612
  0.6 22.2 %copy-start.4 = (bf16[1024,128]{1,0:T(8,128)(2,1)S(1)}, bf16[1024,128]{1,0:T(8,128)(2,1)}, u32[]{:S(2)}) copy-start(bf16[1024,128]{1,0:T(8,128)(2,1)} %param.7) | copy-start | bytes 786436
  19.7 10.0 %collective-permute-start.4 = (bf16[8,8,4096]{2,1,0:T(8,128)(2,1)S(1)}, bf16[8,8,4096]{2,1,0:T(8,128)(2,1)S(1)}, u32[]{:S(2)}, u32[]{:S(2)}) collective-permute-start(bf16[8,8,4096]{2,1,0:T(8,128)(2,1)S(1)} %all_to_all.15), channel_id=1, source_target_pairs={{0,8},{8,0},{16,24},{24,16},{32,40},{40,32},{48,56},{56,48},{64,72... | collective-permute-start | bytes 1572872 | tf_op jit(solution)/shard_map/ppermute | solution.py:213
  22.1 3.6 %collective-permute-start = (bf16[16,2048]{1,0:T(8,128)(2,1)S(1)}, bf16[16,2048]{1,0:T(8,128)(2,1)S(1)}, u32[]{:S(2)}, u32[]{:S(2)}) collective-permute-start(bf16[16,2048]{1,0:T(8,128)(2,1)S(1)} %copy-done.5), channel_id=1, source_target_pairs={{0,4},{1,5},{2,6},{3,7},{4,0},{5,1},{6,2},{7,3},{8,12},{9,13},{10,... | collective-permute-start | bytes 196616 | tf_op jit(solution)/shard_map/ppermute | solution.py:207
  25.8 12.3 %copy-start = (bf16[64,128,128]{2,1,0:T(8,128)(2,1)S(1)}, bf16[64,128,128]{2,1,0:T(8,128)(2,1)}, u32[]{:S(2)}) copy-start(bf16[64,128,128]{2,1,0:T(8,128)(2,1)} %param.9) | copy-start | bytes 6291460
  25.8 12.3 %copy-start.2 = (f32[128]{0:T(128)S(1)}, f32[128]{0:T(128)}, u32[]{:S(2)}) copy-start(f32[128]{0:T(128)} %param.8) | copy-start | bytes 1540
  25.8 7.7 %collective-permute-start.3 = (bf16[2,16,2048]{2,1,0:T(8,128)(2,1)S(1)}, bf16[2,16,2048]{2,1,0:T(8,128)(2,1)S(1)}, u32[]{:S(2)}, u32[]{:S(2)}) collective-permute-start(bf16[2,16,2048]{2,1,0:T(8,128)(2,1)S(1)} %pad_maximum_fusion.1.l0), channel_id=1, source_target_pairs={{0,3},{1,0},{2,1},{3,2},{4,7},{5,4},{6,5},{7,6},{8,11},{9,8},{10,9... | collective-permute-start | bytes 393224 | tf_op jit(solution)/shard_map/ppermute | solution.py:212
  28.6 5.4 %collective-permute-start.2 = (bf16[2,16,2048]{2,1,0:T(8,128)(2,1)S(1)}, bf16[2,16,2048]{2,1,0:T(8,128)(2,1)S(1)}, u32[]{:S(2)}, u32[]{:S(2)}) collective-permute-start(bf16[2,16,2048]{2,1,0:T(8,128)(2,1)S(1)} %pad_maximum_fusion.1.l0), channel_id=1, source_target_pairs={{0,2},{1,3},{2,0},{3,1},{4,6},{5,7},{6,4},{7,5},{8,10},{9,11},{10,... | collective-permute-start | bytes 393224 | tf_op jit(solution)/shard_map/ppermute | solution.py:212
  29.0 9.1 %collective-permute-start.1 = (bf16[2,16,2048]{2,1,0:T(8,128)(2,1)S(1)}, bf16[2,16,2048]{2,1,0:T(8,128)(2,1)S(1)}, u32[]{:S(2)}, u32[]{:S(2)}) collective-permute-start(bf16[2,16,2048]{2,1,0:T(8,128)(2,1)S(1)} %pad_maximum_fusion.1.l0), channel_id=1, source_target_pairs={{0,1},{1,2},{2,3},{3,0},{4,5},{5,6},{6,7},{7,4},{8,9},{9,10},{10,1... | collective-permute-start | bytes 393224 | tf_op jit(solution)/shard_map/ppermute | solution.py:212
  51.3 1.2 %copy-start.1 = (bf16[4096,128]{1,0:T(8,128)(2,1)S(1)}, bf16[4096,128]{1,0:T(8,128)(2,1)}, u32[]{:S(2)}) copy-start(bf16[4096,128]{1,0:T(8,128)(2,1)} %get-tuple-element.18.rt_ref) | copy-start | bytes 3145732
  68.4 10.5 %copy-start.3 = (f32[8,8,4096]{2,1,0:T(8,128)S(1)}, f32[8,8,4096]{2,1,0:T(8,128)}, u32[]{:S(2)}) copy-start(f32[8,8,4096]{2,1,0:T(8,128)} %get-tuple-element.25) | copy-start | bytes 3145732
  68.4 9.4 %collective-permute-start.5 = (bf16[2,16,2048]{2,1,0:T(8,128)(2,1)}, bf16[2,16,2048]{2,1,0:T(8,128)(2,1)S(1)}, u32[]{:S(2)}, u32[]{:S(2)}) collective-permute-start(bf16[2,16,2048]{2,1,0:T(8,128)(2,1)} %get-tuple-element.22), channel_id=1, source_target_pairs={{0,1},{1,2},{2,3},{3,0},{4,5},{5,6},{6,7},{7,4},{8,9},{9,10},{10,1... | collective-permute-start | bytes 393224 | tf_op jit(solution)/shard_map/ppermute | solution.py:238
  68.5 9.3 %collective-permute-start.6 = (bf16[2,16,2048]{2,1,0:T(8,128)(2,1)}, bf16[2,16,2048]{2,1,0:T(8,128)(2,1)S(1)}, u32[]{:S(2)}, u32[]{:S(2)}) collective-permute-start(bf16[2,16,2048]{2,1,0:T(8,128)(2,1)} %get-tuple-element.23), channel_id=1, source_target_pairs={{0,2},{1,3},{2,0},{3,1},{4,6},{5,7},{6,4},{7,5},{8,10},{9,11},{10,... | collective-permute-start | bytes 393224 | tf_op jit(solution)/shard_map/ppermute | solution.py:238
  68.7 9.1 %collective-permute-start.7 = (bf16[2,16,2048]{2,1,0:T(8,128)(2,1)}, bf16[2,16,2048]{2,1,0:T(8,128)(2,1)S(1)}, u32[]{:S(2)}, u32[]{:S(2)}) collective-permute-start(bf16[2,16,2048]{2,1,0:T(8,128)(2,1)} %get-tuple-element.24), channel_id=1, source_target_pairs={{0,3},{1,0},{2,1},{3,2},{4,7},{5,4},{6,5},{7,6},{8,11},{9,8},{10,9... | collective-permute-start | bytes 393224 | tf_op jit(solution)/shard_map/ppermute | solution.py:238
  71.1 7.7 %collective-permute-start.9 = (bf16[8,8,4096]{2,1,0:T(8,128)(2,1)}, bf16[8,8,4096]{2,1,0:T(8,128)(2,1)S(1)}, u32[]{:S(2)}, u32[]{:S(2)}) collective-permute-start(bf16[8,8,4096]{2,1,0:T(8,128)(2,1)} %get-tuple-element.26), channel_id=1, source_target_pairs={{0,8},{8,0},{16,24},{24,16},{32,40},{40,32},{48,56},{56,48},{64,72... | collective-permute-start | bytes 1572872 | tf_op jit(solution)/shard_map/ppermute | solution.py:234
  72.5 19.7 %all-to-all-start.1 = ((f32[128,8,128]{2,1,0:T(8,128)}), f32[128,8,128]{2,1,0:T(8,128)S(1)}, u32[]{:S(2)}, u32[]{:S(2)}) async-start(f32[128,8,128]{2,1,0:T(8,128)} %bitcast.21), calls=%async_computation.1 | async-start | bytes 1048576 | tf_op jit(solution)/shard_map/all_to_all | solution.py:224
  78.9 18.9 %collective-permute-start.10 = (bf16[2,8,4096]{2,1,0:T(8,128)(2,1)S(1)}, bf16[2,8,4096]{2,1,0:T(8,128)(2,1)S(1)}, u32[]{:S(2)}, u32[]{:S(2)}) collective-permute-start(bf16[2,8,4096]{2,1,0:T(8,128)(2,1)S(1)} %get-tuple-element.29), channel_id=1, source_target_pairs={{0,32},{8,40},{16,48},{24,56},{32,64},{40,72},{48,80},{56,88},{64,... | collective-permute-start | bytes 393224 | tf_op jit(solution)/shard_map/ppermute | solution.py:237
  80.4 17.5 %collective-permute-start.12 = (bf16[2,8,4096]{2,1,0:T(8,128)(2,1)S(1)}, bf16[2,8,4096]{2,1,0:T(8,128)(2,1)S(1)}, u32[]{:S(2)}, u32[]{:S(2)}) collective-permute-start(bf16[2,8,4096]{2,1,0:T(8,128)(2,1)S(1)} %get-tuple-element.30), channel_id=1, source_target_pairs={{0,96},{8,104},{16,112},{24,120},{32,0},{40,8},{48,16},{56,24},{64... | collective-permute-start | bytes 393224 | tf_op jit(solution)/shard_map/ppermute | solution.py:237
  81.7 16.2 %collective-permute-start.11 = (bf16[2,8,4096]{2,1,0:T(8,128)(2,1)S(1)}, bf16[2,8,4096]{2,1,0:T(8,128)(2,1)S(1)}, u32[]{:S(2)}, u32[]{:S(2)}) collective-permute-start(bf16[2,8,4096]{2,1,0:T(8,128)(2,1)S(1)} %get-tuple-element.31), channel_id=1, source_target_pairs={{0,64},{8,72},{16,80},{24,88},{32,96},{40,104},{48,112},{56,120},{... | collective-permute-start | bytes 393224 | tf_op jit(solution)/shard_map/ppermute | solution.py:237
  83.3 18.1 %collective-permute-start.8 = (bf16[16,2048]{1,0:T(8,128)(2,1)S(1)}, bf16[16,2048]{1,0:T(8,128)(2,1)S(1)}, u32[]{:S(2)}, u32[]{:S(2)}) collective-permute-start(bf16[16,2048]{1,0:T(8,128)(2,1)S(1)} %fusion.4), channel_id=1, source_target_pairs={{0,4},{1,5},{2,6},{3,7},{4,0},{5,1},{6,2},{7,3},{8,12},{9,13},{10,... | collective-permute-start | bytes 196616 | tf_op jit(solution)/shard_map/ppermute | solution.py:241
  93.4 19.2 %all-to-all-start.2 = ((f32[128,1,1152]{2,1,0:T(1,128)}), f32[128,1,1152]{2,1,0:T(1,128)S(1)}, u32[]{:S(2)}, u32[]{:S(2)}) async-start(f32[128,1,1152]{2,1,0:T(1,128)} %broadcast_in_dim.21), calls=%async_computation.2 | async-start | bytes 1179648 | tf_op jit(solution)/shard_map/all_to_all | solution.py:230
  98.0 8.3 %collective-permute-start.13 = (bf16[8,4096]{1,0:T(8,128)(2,1)S(1)}, bf16[8,4096]{1,0:T(8,128)(2,1)S(1)}, u32[]{:S(2)}, u32[]{:S(2)}) collective-permute-start(bf16[8,4096]{1,0:T(8,128)(2,1)S(1)} %fusion.6), channel_id=1, source_target_pairs={{0,16},{8,24},{16,0},{24,8},{32,48},{40,56},{48,32},{56,40},{64,80... | collective-permute-start | bytes 196616 | tf_op jit(solution)/shard_map/ppermute | solution.py:244

commit v3 on v2

--- a/solution.py
+++ b/solution.py
@@ -11,6 +11,7 @@
 FB = 16
 IB = 8
 EB = 8
+GB = 1024
 BF = jnp.bfloat16
 F32 = jnp.float32
 
@@ -48,16 +49,35 @@
     return l_s[...].reshape(l_s.shape[0] * l_s.shape[1], l_s.shape[2])
 
 
-def forward_body(l0, l1, l2, l3, r_ref, d_ref, wt_ref, b_ref, p_ref, gw_ref, gb_ref, rt_ref, l_s):
+def forward_body(*refs):
+    l_refs, refs = refs[:NY], refs[NY:]
+    own, other, refs = refs[:NX], refs[NX : 2 * NX], refs[2 * NX :]
+    d_ref, wt_ref, b_ref, p_ref, out_ref, rt_ref, l_s, r_s, gw_s, gb_s = refs
     k = pl.program_id(0)
     nj = d_ref.shape[0] // FB
-    left = left_block((l0, l1, l2, l3), l_s).T
-    scale = 1.0 / left.shape[1]
+
+    @pl.when(k == 0)
+    def _():
+        gw_s[...] = jnp.zeros_like(gw_s)
+        gb_s[...] = jnp.zeros_like(gb_s)
+        row = lax.axis_index("row")
+        x, zh, core = row // (NZ * NC), row // NC % NZ, row % NC
+        for d in range(NX):
+            for b in range(NZ):
+                at = ((x + NX - d) % NX * NZ + (zh + b) % NZ) * NC
+                r_s[at + core] = own[d][b]
+                r_s[at + 1 - core] = other[d][b]
+
+    left = left_block(l_refs, l_s).T
+    seqs = left.shape[1]
+    scale = 1.0 / seqs
     part = rt_ref.shape[0]
-    rt_ref[...] = r_ref[:, pl.ds(pl.multiple_of(k * part, part), part)].T
+    turn = r_s[:, :, pl.ds(pl.multiple_of(k * part, part), part)]
+    rt_ref[...] = turn.reshape(seqs, part).T
     rows = []
     for eb in range(CL // EB):
-        t = dot(left, r_ref[:, eb * EB * nj : (eb + 1) * EB * nj], 1, 0)
+        right = r_s[:, :, eb * EB * nj : (eb + 1) * EB * nj].reshape(seqs, EB * nj)
+        t = dot(left, right, 1, 0)
         t = (t * scale).astype(BF)
         for e1 in range(EB):
             rows.append(
@@ -70,15 +90,28 @@
     gw = dot(outer, d_ref[...], 1, 0)
     gb = jnp.sum(d_ref[...].astype(F32).reshape(-1, 8, CP), axis=0)
 
-    @pl.when(k == 0)
-    def _():
-        gw_ref[...] = gw
-        gb_ref[...] = gb
-
-    @pl.when(k != 0)
-    def _():
-        gw_ref[...] += gw
-        gb_ref[...] += gb
+    gw_s[...] += gw
+    gb_s[...] += gb
+
+    @pl.when(k == pl.num_programs(0) - 1)
+    def _():
+        total = jnp.sum(gb_s[...], axis=0, keepdims=True)
+        high = total.astype(BF).astype(F32)
+        middle = (total - high).astype(BF).astype(F32)
+        at = lax.broadcasted_iota(jnp.int32, gb_s.shape, 0)
+        tail = jnp.where(at == 0, high, jnp.where(at == 1, middle, total - high - middle))
+        tail = jnp.where(at < 3, tail, 0.0).astype(BF)
+        ndev, rows = out_ref.shape[0], out_ref.shape[1] - 8
+        for dev in range(ndev):
+            c, e = divmod(dev * rows, CL)
+            out_ref[dev, :rows] = gw_s[pl.ds(e * CL + c, rows, stride=CL), :].astype(BF)
+            out_ref[dev, rows:] = tail
+
+
+def weight_body(x_ref, gw_ref, gb_ref):
+    total = jnp.sum(x_ref[...].astype(F32), axis=0)
+    gw_ref[...] = jnp.broadcast_to(total[None, :-8], gw_ref.shape)
+    gb_ref[...] = jnp.sum(total[-8:], axis=0, keepdims=True)
 
 
 def backward_body(
@@ -86,6 +119,11 @@
 ):
     k = pl.program_id(0)
     nj = d_ref.shape[0] // IB
+
+    @pl.when(k == 0)
+    def _():
+        acc[...] = jnp.zeros_like(acc)
+
     left = left_block((l0, l1, l2, l3), l_s)
     scale = 1.0 / left.shape[0]
     rows = []
@@ -104,15 +142,9 @@
     for d, out in enumerate((g0, g1, g2, g3)):
         for b in range(NZ):
             out[b] = gl_s[(z + b) % NZ * NY + (y + d) % NY].astype(out.dtype)
-    gr = dot(left, grad, 1, 0).reshape(acc.shape)
-
-    @pl.when(k == 0)
-    def _():
-        acc[...] = gr
-
-    @pl.when(k != 0)
-    def _():
-        acc[...] += gr
+    for at in range(0, CL * nj, GB):
+        gr = dot(left, grad[:, at : at + GB], 1, 0)
+        acc[:, :, at : at + GB] += gr.reshape(acc.shape[:2] + (GB,))
 
     @pl.when(k == pl.num_programs(0) - 1)
     def _():
@@ -129,36 +161,40 @@
     return pltpu.CompilerParams(dimension_semantics=("arbitrary",), vmem_limit_bytes=mib << 20)
 
 
-def forward(pieces, right, dpair, wt, bias):
+def forward(pieces, own, other, dpair, wt, bias, ndev):
     scol, width = pieces[0].shape[1:]
-    seqs, nj = right.shape[0], right.shape[1] // CL
+    srow = own[0].shape[1]
+    seqs, nj = scol * NZ * NY, own[0].shape[2] // CL
     n = width // (FB * CL)
     return pl.pallas_call(
         forward_body,
         grid=(n,),
         out_shape=(
             jax.ShapeDtypeStruct((n * FB * nj, CP), BF),
-            pltpu.HBM((CL * CL, CP), F32),
-            jax.ShapeDtypeStruct((8, CP), F32),
+            pltpu.HBM((ndev, CL * CL // ndev + 8, CP), BF),
             pltpu.HBM((CL * nj, seqs), BF),
         ),
         in_specs=[pl.BlockSpec((NZ, scol, FB * CL), lambda k: (0, 0, k))] * NY
+        + [whole(NZ, srow, CL * nj)] * (2 * NX)
         + [
-            whole(seqs, CL * nj),
             pl.BlockSpec((FB * nj, CP), lambda k: (k, 0)),
             whole(CP, CL * CL),
             whole(1, CP),
         ],
         out_specs=(
             pl.BlockSpec((FB * nj, CP), lambda k: (k, 0)),
-            whole(CL * CL, CP),
-            whole(8, CP),
+            whole(ndev, CL * CL // ndev + 8, CP),
             pl.BlockSpec((CL * nj // n, seqs), lambda k: (k, 0)),
         ),
-        scratch_shapes=[pltpu.VMEM((NZ * NY, scol, FB * CL), BF)],
+        scratch_shapes=[
+            pltpu.VMEM((NZ * NY, scol, FB * CL), BF),
+            pltpu.VMEM((NX * NZ * NC, srow, CL * nj), BF),
+            pltpu.VMEM((CL * CL, CP), F32),
+            pltpu.VMEM((8, CP), F32),
+        ],
         compiler_params=params(40),
         name="forward",
-    )(*pieces, right, dpair, wt, bias)
+    )(*pieces, *own, *other, dpair, wt, bias)
 
 
 def backward(pieces, right_t, dpair, w):
@@ -199,37 +235,33 @@
 def shards(left, right, weight, bias, cotangent):
     ndev = lax.axis_size("row") * lax.axis_size("col")
     srow = right.shape[0]
-    seqs = srow * lax.axis_size("row")
     ni, nj = cotangent.shape[0], cotangent.shape[1]
-    same_core = [[xz * NC + c for xz in range(NX * NZ)] for c in range(NC)]
-    core = lax.axis_index("row") & 1
 
     other = lax.ppermute(left, "col", col_shift(1, 0))
-    mine = right.reshape(srow, nj, CL).transpose(0, 2, 1).reshape(1, srow, CL * nj)
-    mine = jnp.broadcast_to(mine, (NX * NZ, srow, CL * nj))
-    mine = lax.all_to_all(mine, "row", 0, 0, tiled=True, axis_index_groups=same_core)
+    mine = right.reshape(srow, nj, CL).transpose(0, 2, 1).reshape(srow, CL * nj)
+    theirs = lax.ppermute(mine, "row", row_shift(0, 1, 0))
     pair = jnp.stack([left, other])
     pieces = [pair] + [lax.ppermute(pair, "col", col_shift(0, d)) for d in range(1, NY)]
-    theirs = lax.ppermute(mine, "row", row_shift(0, 0, 1))
-    first = jnp.where(core == 0, mine, theirs)
-    second = jnp.where(core == 0, theirs, mine)
-    right_full = jnp.stack([first, second], axis=1).reshape(seqs, CL * nj)
+    pair = jnp.stack([mine, theirs])
+    mine = [pair] + [lax.ppermute(pair, "row", row_shift(d, 0, 0)) for d in range(1, NX)]
+    theirs = [lax.ppermute(p, "row", row_shift(0, 0, 1)) for p in mine]
 
     dpair = cotangent.reshape(ni * nj, CP)
     w = weight.reshape(CL, CL, CP).transpose(1, 0, 2).reshape(CL * CL, CP)
-    pair_update, gw, gb, right_t = forward(pieces, right_full, dpair, w.T, bias.reshape(1, CP))
-
-    rows = CL * CL // ndev
-    gw, dpair = lax.optimization_barrier((gw, dpair))
-    gw = lax.all_to_all(gw.reshape(ndev, rows, CP), ("row", "col"), 0, 0, tiled=True)
-    gw = jnp.concatenate([jnp.sum(gw, axis=0), jnp.sum(gb, axis=0, keepdims=True)], axis=0)
-
+    wt = w.T
+    pair_update, share, right_t = forward(
+        pieces, mine, theirs, dpair, wt, bias.reshape(1, CP), ndev
+    )
+    share, dpair = lax.optimization_barrier((share, dpair))
+    share = lax.all_to_all(share, ("row", "col"), 0, 0, tiled=True)
     l0, l1, l2, l3, keep, send = backward(pieces, right_t, dpair, w)
-
-    gw = jnp.broadcast_to(gw.reshape(1, 1, (rows + 1) * CP), (ndev, 1, (rows + 1) * CP))
-    gw = lax.all_to_all(gw, ("row", "col"), 0, 0, tiled=True)
-    grad_b = jnp.sum(gw[:, 0, rows * CP :], axis=0)
-    grad_w = gw[:, 0, : rows * CP].reshape(CL, CL, CP).transpose(1, 0, 2).reshape(CL * CL, CP)
+    own, grad_b = pl.pallas_call(
+        weight_body,
+        out_shape=(pltpu.HBM((ndev, CL * CL // ndev, CP), F32), jax.ShapeDtypeStruct((1, CP), F32)),
+        name="weight",
+    )(share)
+    grad_w = lax.all_to_all(own, ("row", "col"), 0, 0, tiled=True).reshape(CL * CL, CP)
+    grad_b = grad_b.reshape(CP)
 
     got = lax.ppermute(send, "row", row_shift(0, 0, 1))
     part = [keep[NZ * d : NZ * (d + 1)] + got[NZ * d : NZ * (d + 1)].astype(F32) for d in range(NX)]

time: 115 us -> 104 us (0.904)
  blocking collectives: 17.7 us -> 0 us
  starting transfers between devices: 30.1 us -> 46.1 us
  waiting for transfers between devices: 27.7 us -> 16.8 us
  Pallas kernels: 29.1 us -> 31.1 us
    all_to_all x1 -> x0, blocking collectives: 17.7 us -> none  [shards(): lax.all_to_all(mine, 'row', 0, 0, tiled=True, axis_index_groups=same_core)]
    ppermute x1 -> x8, starting transfers between devices: 2.45 us -> 13.5 us  [the longest x4 5.19 us: shards(): theirs = [lax.ppermute(p, 'row', row_shift(0, 0, 1)) for p in mine]]
    ppermute x3, waiting for transfers between devices: 8.23 us -> 0.01 us  [shards(): lax.ppermute(pair, 'col', col_shift(0, d))]
    all_to_all x2, starting transfers between devices: 9.72 us -> 12.9 us  [the longest x1 7.83 us: shards(): share = lax.all_to_all(share, ('row', 'col'), 0, 0, tiled=True)]
    ppermute x1, waiting for transfers between devices: 2.64 us -> 0.01 us  [shards(): other = lax.ppermute(left, 'col', col_shift(1, 0))]
    pallas_call x0 -> x1, Pallas kernels: none -> 2 us  [shards(): pl.pallas_call(weight_body, out_shape=(pltpu.HBM((ndev, CL * CL // ndev,...]
    ppermute x1, starting transfers between devices: 0.74 us -> 2.53 us  [shards(): other = lax.ppermute(left, 'col', col_shift(1, 0))]
    unnamed x13 -> x11, local copies, waits for them, and re-layouts: 1.28 us -> 2.82 us
  transfers between devices with their start and end apart: 16 -> 23, of which waited for: 7 -> 4; matrix products, arithmetic and copies ran while one was open for 4% -> 6% of each run, Pallas kernels for 0% -> 2%
where the time goes in v3:
time: 104 us
  starting transfers between devices  46.1 us (44%)
  Pallas kernels  31.1 us (30%)
  waiting for transfers between devices  16.8 us (16%)
  local copies, waits for them, and re-layouts  6.35 us (6%)
  other arithmetic  2.69 us (3%)
    pallas_call x1, Pallas kernels, forward(): pl.pallas_call(forward_body, grid=(n,), out_shape=(jax.ShapeDtypeStruct((...  14.7 us
    pallas_call x1, Pallas kernels, backward(): pl.pallas_call(backward_body, grid=(n,), out_shape=(pltpu.HBM((NZ, scol,...  14.4 us
    all_to_all x1, starting transfers between devices, shards(): share = lax.all_to_all(share, ('row', 'col'), 0, 0, tiled=True)  7.83 us
    all_to_all x1, waiting for transfers between devices, shards(): share = lax.all_to_all(share, ('row', 'col'), 0, 0, tiled=True)  7.81 us
    all_to_all x1, waiting for transfers between devices, shards(): lax.all_to_all(own, ('row', 'col'), 0, 0, tiled=True).reshape(CL * CL, CP)  5.52 us
    ppermute x4, starting transfers between devices, shards(): theirs = [lax.ppermute(p, 'row', row_shift(0, 0, 1)) for p in mine]  5.19 us
    all_to_all x1, starting transfers between devices, shards(): lax.all_to_all(own, ('row', 'col'), 0, 0, tiled=True).reshape(CL * CL, CP)  5.07 us
    ppermute x3, starting transfers between devices, shards(): lax.ppermute(pair, 'col', col_shift(0, d))  5.05 us
  transfers between devices with their start and end apart: 23, of which 4 were waited for; matrix products, arithmetic and copies ran while one was open for 6% of the time, Pallas kernels for 2%

profile of v3, /device:TPU:1, one launch (start us, length us, event | category | flops | bytes accessed | tf_op | source)
XLA Modules:
  0.0 103.9 jit_solution(16739242230891853158)
XLA Ops:
  0.7 2.5 %collective-permute-start = (bf16[16,2048]{1,0:T(8,128)(2,1)}, bf16[16,2048]{1,0:T(8,128)(2,1)S(1)}, u32[]{:S(2)}, u32[]{:S(2)}) collective-permute-start(bf16[16,2048]{1,0:T(8,128)(2,1)} %param.5), channel_id=1, source_target_pairs={{0,4},{1,5},{2,6},{3,7},{4,0},{5,1},{6,2},{7,3},{8,12},{9,13},{10,... | collective-permute-start | bytes 196616 | tf_op jit(solution)/shard_map/ppermute | solution.py:240
  3.2 1.1 %reshape.45 = bf16[8,128,32]{2,1,0:T(8,128)(2,1)S(1)} reshape(bf16[8,4096]{1,0:T(8,128)(2,1)} %param.6) | data formatting | bytes 131072 | tf_op jit(solution)/shard_map/reshape | solution.py:241
  4.4 3.4 %collective-permute-start.4 = (bf16[8,4096]{1,0:T(8,128)(2,1)S(1)}, bf16[8,4096]{1,0:T(8,128)(2,1)S(1)}, u32[]{:S(2)}, u32[]{:S(2)}) collective-permute-start(bf16[8,4096]{1,0:T(8,128)(2,1)S(1)} %bitcast.47), channel_id=1, source_target_pairs={{0,16},{8,24},{16,0},{24,8},{32,48},{40,56},{48,32},{56,40},{64,80... | collective-permute-start | bytes 196616 | tf_op jit(solution)/shard_map/ppermute | solution.py:242
  7.8 0.9 pad_maximum_fusion.refs_0_.l0
  8.6 1.4 %collective-permute-start.1 = (bf16[2,16,2048]{2,1,0:T(8,128)(2,1)S(1)}, bf16[2,16,2048]{2,1,0:T(8,128)(2,1)S(1)}, u32[]{:S(2)}, u32[]{:S(2)}) collective-permute-start(bf16[2,16,2048]{2,1,0:T(8,128)(2,1)S(1)} %pad_maximum_fusion.refs_0_.l0), channel_id=1, source_target_pairs={{0,1},{1,2},{2,3},{3,0},{4,5},{5,6},{6,7},{7,4},{8,9},{9,10},{10,1... | collective-permute-start | bytes 393224 | tf_op jit(solution)/shard_map/ppermute | solution.py:244
  10.0 2.6 %collective-permute-start.2 = (bf16[2,16,2048]{2,1,0:T(8,128)(2,1)S(1)}, bf16[2,16,2048]{2,1,0:T(8,128)(2,1)S(1)}, u32[]{:S(2)}, u32[]{:S(2)}) collective-permute-start(bf16[2,16,2048]{2,1,0:T(8,128)(2,1)S(1)} %pad_maximum_fusion.refs_0_.l0), channel_id=1, source_target_pairs={{0,2},{1,3},{2,0},{3,1},{4,6},{5,7},{6,4},{7,5},{8,10},{9,11},{10,... | collective-permute-start | bytes 393224 | tf_op jit(solution)/shard_map/ppermute | solution.py:244
  12.7 1.3 %collective-permute-start.5 = (bf16[2,8,4096]{2,1,0:T(8,128)(2,1)S(1)}, bf16[2,8,4096]{2,1,0:T(8,128)(2,1)S(1)}, u32[]{:S(2)}, u32[]{:S(2)}) collective-permute-start(bf16[2,8,4096]{2,1,0:T(8,128)(2,1)S(1)} %pad_maximum_fusion.1.refs_4_), channel_id=1, source_target_pairs={{0,32},{8,40},{16,48},{24,56},{32,64},{40,72},{48,80},{56,88},{64,... | collective-permute-start | bytes 393224 | tf_op jit(solution)/shard_map/ppermute | solution.py:246
  13.9 2.5 %collective-permute-start.6 = (bf16[2,8,4096]{2,1,0:T(8,128)(2,1)S(1)}, bf16[2,8,4096]{2,1,0:T(8,128)(2,1)S(1)}, u32[]{:S(2)}, u32[]{:S(2)}) collective-permute-start(bf16[2,8,4096]{2,1,0:T(8,128)(2,1)S(1)} %pad_maximum_fusion.1.refs_4_), channel_id=1, source_target_pairs={{0,64},{8,72},{16,80},{24,88},{32,96},{40,104},{48,112},{56,120},{... | collective-permute-start | bytes 393224 | tf_op jit(solution)/shard_map/ppermute | solution.py:246
  16.4 1.2 %collective-permute-start.7 = (bf16[2,8,4096]{2,1,0:T(8,128)(2,1)S(1)}, bf16[2,8,4096]{2,1,0:T(8,128)(2,1)}, u32[]{:S(2)}, u32[]{:S(2)}) collective-permute-start(bf16[2,8,4096]{2,1,0:T(8,128)(2,1)S(1)} %pad_maximum_fusion.1.refs_4_), channel_id=1, source_target_pairs={{0,96},{8,104},{16,112},{24,120},{32,0},{40,8},{48,16},{56,24},{64... | collective-permute-start | bytes 393224 | tf_op jit(solution)/shard_map/ppermute | solution.py:246
  17.5 1.1 %collective-permute-start.3 = (bf16[2,16,2048]{2,1,0:T(8,128)(2,1)S(1)}, bf16[2,16,2048]{2,1,0:T(8,128)(2,1)S(1)}, u32[]{:S(2)}, u32[]{:S(2)}) collective-permute-start(bf16[2,16,2048]{2,1,0:T(8,128)(2,1)S(1)} %pad_maximum_fusion.refs_0_.l0), channel_id=1, source_target_pairs={{0,3},{1,0},{2,1},{3,2},{4,7},{5,4},{6,5},{7,6},{8,11},{9,8},{10,9... | collective-permute-start | bytes 393224 | tf_op jit(solution)/shard_map/ppermute | solution.py:244
  18.6 2.9 %collective-permute-start.8 = (bf16[2,8,4096]{2,1,0:T(8,128)(2,1)S(1)}, bf16[2,8,4096]{2,1,0:T(8,128)(2,1)}, u32[]{:S(2)}, u32[]{:S(2)}) collective-permute-start(bf16[2,8,4096]{2,1,0:T(8,128)(2,1)S(1)} %pad_maximum_fusion.1.refs_4_), channel_id=1, source_target_pairs={{0,8},{8,0},{16,24},{24,16},{32,40},{40,32},{48,56},{56,48},{64,72... | collective-permute-start | bytes 393224 | tf_op jit(solution)/shard_map/ppermute | solution.py:247
  22.1 1.5 %collective-permute-start.10 = (bf16[2,8,4096]{2,1,0:T(8,128)(2,1)S(1)}, bf16[2,8,4096]{2,1,0:T(8,128)(2,1)}, u32[]{:S(2)}, u32[]{:S(2)}) collective-permute-start(bf16[2,8,4096]{2,1,0:T(8,128)(2,1)S(1)} %collective-permute-done.6.refs_6_), channel_id=1, source_target_pairs={{0,8},{8,0},{16,24},{24,16},{32,40},{40,32},{48,56},{56,48},{64,72... | collective-permute-start | bytes 393224 | tf_op jit(solution)/shard_map/ppermute | solution.py:247
  23.8 1.1 %copy.16 = bf16[32,32,128]{2,0,1:T(8,128)(2,1)S(1)} copy(bf16[32,32,128]{2,1,0:T(8,128)(2,1)} %bitcast.46) | data formatting | bytes 524288 | tf_op jit(solution)/shard_map/reshape | solution.py:250
  25.3 14.7 %forward.1 = (bf16[8192,128]{1,0:T(8,128)(2,1)}, bf16[128,16,128]{2,1,0:T(8,128)(2,1)}, bf16[4096,128]{1,0:T(8,128)(2,1)}) custom-call(bf16[2,16,2048]{2,1,0:T(8,128)(2,1)S(1)} %pad_maximum_fusion.refs_0_.l0, bf16[2,16,2048]{2,1,0:T(8,128)(2,1)S(1)} %collective-permute-done.1.refs_1_.l1, bf16[2,16,2048]{2,1,0:T(8,128)(2,1)S(1)} %collective-permute-done.2.refs_2_.l2, ...), custom_call_target="tpu_custom_call" | custom-call | tf_op jit(solution)/shard_map/forward/pallas_call | solution.py:169
  40.1 1.2 %copy-done.1 = bf16[4096,128]{1,0:T(8,128)(2,1)S(1)} copy-done((bf16[4096,128]{1,0:T(8,128)(2,1)S(1)}, bf16[4096,128]{1,0:T(8,128)(2,1)}, u32[]{:S(2)}) %copy-start.1) | copy-done | bytes 1048600
  41.3 14.4 %backward.1 = (f32[2,16,2048]{2,1,0:T(8,128)}, bf16[2,16,2048]{2,1,0:T(8,128)(2,1)}, bf16[2,16,2048]{2,1,0:T(8,128)(2,1)}, bf16[2,16,2048]{2,1,0:T(8,128)(2,1)},...) custom-call(bf16[2,16,2048]{2,1,0:T(8,128)(2,1)S(1)} %pad_maximum_fusion.refs_0_.l0, ...), custom_call_target="tpu_custom_call" | custom-call | tf_op jit(solution)/shard_map/backward/pallas_call | solution.py:207
  55.7 1.1 %collective-permute-start.14 = (bf16[2,16,2048]{2,1,0:T(8,128)(2,1)}, bf16[2,16,2048]{2,1,0:T(8,128)(2,1)S(1)}, u32[]{:S(2)}, u32[]{:S(2)}) collective-permute-start(bf16[2,16,2048]{2,1,0:T(8,128)(2,1)} %get-tuple-element.25), channel_id=1, source_target_pairs={{0,3},{1,0},{2,1},{3,2},{4,7},{5,4},{6,5},{7,6},{8,11},{9,8},{10,9... | collective-permute-start | bytes 393224 | tf_op jit(solution)/shard_map/ppermute | solution.py:270
  57.5 1.6 %collective-permute-start.16 = (bf16[8,8,4096]{2,1,0:T(8,128)(2,1)}, bf16[8,8,4096]{2,1,0:T(8,128)(2,1)S(1)}, u32[]{:S(2)}, u32[]{:S(2)}) collective-permute-start(bf16[8,8,4096]{2,1,0:T(8,128)(2,1)} %get-tuple-element.27), channel_id=1, source_target_pairs={{0,8},{8,0},{16,24},{24,16},{32,40},{40,32},{48,56},{56,48},{64,72... | collective-permute-start | bytes 1572872 | tf_op jit(solution)/shard_map/ppermute | solution.py:266
  59.1 7.8 %all-to-all-start = ((bf16[128,16,128]{2,1,0:T(8,128)(2,1)}), bf16[128,16,128]{2,1,0:T(8,128)(2,1)S(1)}, u32[]{:S(2)}, u32[]{:S(2)}) async-start(bf16[128,16,128]{2,1,0:T(8,128)(2,1)} %get-tuple-element.28), calls=%async_computation | async-start | bytes 1048576 | tf_op jit(solution)/shard_map/all_to_all | solution.py:256
  67.0 1.0 add_add_fusion.1
  68.1 2.8 %collective-permute-start.19 = (bf16[2,8,4096]{2,1,0:T(8,128)(2,1)S(1)}, bf16[2,8,4096]{2,1,0:T(8,128)(2,1)S(1)}, u32[]{:S(2)}, u32[]{:S(2)}) collective-permute-start(bf16[2,8,4096]{2,1,0:T(8,128)(2,1)S(1)} %get-tuple-element.32), channel_id=1, source_target_pairs={{0,96},{8,104},{16,112},{24,120},{32,0},{40,8},{48,16},{56,24},{64... | collective-permute-start | bytes 393224 | tf_op jit(solution)/shard_map/ppermute | solution.py:269
  72.1 1.4 %collective-permute-start.15 = (bf16[16,2048]{1,0:T(8,128)(2,1)S(1)}, bf16[16,2048]{1,0:T(8,128)(2,1)S(1)}, u32[]{:S(2)}, u32[]{:S(2)}) collective-permute-start(bf16[16,2048]{1,0:T(8,128)(2,1)S(1)} %fusion.4), channel_id=1, source_target_pairs={{0,4},{1,5},{2,6},{3,7},{4,0},{5,1},{6,2},{7,3},{8,12},{9,13},{10,... | collective-permute-start | bytes 196616 | tf_op jit(solution)/shard_map/ppermute | solution.py:273
  73.5 7.8 %all-to-all-done.x_ref = bf16[128,16,128]{2,1,0:T(8,128)(2,1)S(1)} async-done(((bf16[128,16,128]{2,1,0:T(8,128)(2,1)}), bf16[128,16,128]{2,1,0:T(8,128)(2,1)S(1)}, u32[]{:S(2)}, u32[]{:S(2)}) %all-to-all-start) | async-done | bytes 524320 | tf_op jit(solution)/shard_map/all_to_all | solution.py:256
  81.3 0.8 copy-done.3
  82.1 2.0 %weight.1 = (f32[128,8,128]{2,1,0:T(8,128)}, f32[1,128]{1,0:T(1,128)}) custom-call(bf16[128,16,128]{2,1,0:T(8,128)(2,1)} %copy-done.3), custom_call_target="tpu_custom_call" | custom-call | tf_op jit(solution)/shard_map/weight/pallas_call | solution.py:258
  84.1 5.1 %all-to-all-start.1 = ((f32[128,8,128]{2,1,0:T(8,128)}), f32[128,8,128]{2,1,0:T(8,128)S(1)}, u32[]{:S(2)}, u32[]{:S(2)}) async-start(f32[128,8,128]{2,1,0:T(8,128)} %get-tuple-element.29), calls=%async_computation.1 | async-start | bytes 1048576 | tf_op jit(solution)/shard_map/all_to_all | solution.py:263
  89.3 3.3 %collective-permute-start.20 = (bf16[8,4096]{1,0:T(8,128)(2,1)S(1)}, bf16[8,4096]{1,0:T(8,128)(2,1)S(1)}, u32[]{:S(2)}, u32[]{:S(2)}) collective-permute-start(bf16[8,4096]{1,0:T(8,128)(2,1)S(1)} %fusion.6), channel_id=1, source_target_pairs={{0,16},{8,24},{16,0},{24,8},{32,48},{40,56},{48,32},{56,40},{64,80... | collective-permute-start | bytes 196616 | tf_op jit(solution)/shard_map/ppermute | solution.py:276
  92.7 0.6 fusion.3
  93.3 3.2 %collective-permute-done.20 = bf16[8,4096]{1,0:T(8,128)(2,1)S(1)} collective-permute-done((bf16[8,4096]{1,0:T(8,128)(2,1)S(1)}, bf16[8,4096]{1,0:T(8,128)(2,1)S(1)}, u32[]{:S(2)}, u32[]{:S(2)}) %collective-permute-start.20) | collective-permute-done | bytes 65568 | tf_op jit(solution)/shard_map/ppermute | solution.py:276
  96.7 0.9 reshape.53
  97.6 5.5 %all-to-all-done.1 = f32[128,8,128]{2,1,0:T(8,128)S(1)} async-done(((f32[128,8,128]{2,1,0:T(8,128)}), f32[128,8,128]{2,1,0:T(8,128)S(1)}, u32[]{:S(2)}, u32[]{:S(2)}) %all-to-all-start.1) | async-done | bytes 524320 | tf_op jit(solution)/shard_map/all_to_all | solution.py:263
  103.2 0.8 copy.20
  (43 shorter events, 3.6 us)
Async XLA Ops:
  0.6 24.7 %copy-start = (bf16[64,128,128]{2,1,0:T(8,128)(2,1)S(1)}, bf16[64,128,128]{2,1,0:T(8,128)(2,1)}, u32[]{:S(2)}) copy-start(bf16[64,128,128]{2,1,0:T(8,128)(2,1)} %param.9) | copy-start | bytes 6291460
  0.6 24.7 %copy-start.2 = (f32[128]{0:T(128)S(1)}, f32[128]{0:T(128)}, u32[]{:S(2)}) copy-start(f32[128]{0:T(128)} %param.8) | copy-start | bytes 1540
  0.7 7.1 %collective-permute-start = (bf16[16,2048]{1,0:T(8,128)(2,1)}, bf16[16,2048]{1,0:T(8,128)(2,1)S(1)}, u32[]{:S(2)}, u32[]{:S(2)}) collective-permute-start(bf16[16,2048]{1,0:T(8,128)(2,1)} %param.5), channel_id=1, source_target_pairs={{0,4},{1,5},{2,6},{3,7},{4,0},{5,1},{6,2},{7,3},{8,12},{9,13},{10,... | collective-permute-start | bytes 196616 | tf_op jit(solution)/shard_map/ppermute | solution.py:240
  4.4 8.2 %collective-permute-start.4 = (bf16[8,4096]{1,0:T(8,128)(2,1)S(1)}, bf16[8,4096]{1,0:T(8,128)(2,1)S(1)}, u32[]{:S(2)}, u32[]{:S(2)}) collective-permute-start(bf16[8,4096]{1,0:T(8,128)(2,1)S(1)} %bitcast.47), channel_id=1, source_target_pairs={{0,16},{8,24},{16,0},{24,8},{32,48},{40,56},{48,32},{56,40},{64,80... | collective-permute-start | bytes 196616 | tf_op jit(solution)/shard_map/ppermute | solution.py:242
  8.6 8.9 %collective-permute-start.1 = (bf16[2,16,2048]{2,1,0:T(8,128)(2,1)S(1)}, bf16[2,16,2048]{2,1,0:T(8,128)(2,1)S(1)}, u32[]{:S(2)}, u32[]{:S(2)}) collective-permute-start(bf16[2,16,2048]{2,1,0:T(8,128)(2,1)S(1)} %pad_maximum_fusion.refs_0_.l0), channel_id=1, source_target_pairs={{0,1},{1,2},{2,3},{3,0},{4,5},{5,6},{6,7},{7,4},{8,9},{9,10},{10,1... | collective-permute-start | bytes 393224 | tf_op jit(solution)/shard_map/ppermute | solution.py:244
  10.0 8.6 %collective-permute-start.2 = (bf16[2,16,2048]{2,1,0:T(8,128)(2,1)S(1)}, bf16[2,16,2048]{2,1,0:T(8,128)(2,1)S(1)}, u32[]{:S(2)}, u32[]{:S(2)}) collective-permute-start(bf16[2,16,2048]{2,1,0:T(8,128)(2,1)S(1)} %pad_maximum_fusion.refs_0_.l0), channel_id=1, source_target_pairs={{0,2},{1,3},{2,0},{3,1},{4,6},{5,7},{6,4},{7,5},{8,10},{9,11},{10,... | collective-permute-start | bytes 393224 | tf_op jit(solution)/shard_map/ppermute | solution.py:244
  12.7 8.9 %collective-permute-start.5 = (bf16[2,8,4096]{2,1,0:T(8,128)(2,1)S(1)}, bf16[2,8,4096]{2,1,0:T(8,128)(2,1)S(1)}, u32[]{:S(2)}, u32[]{:S(2)}) collective-permute-start(bf16[2,8,4096]{2,1,0:T(8,128)(2,1)S(1)} %pad_maximum_fusion.1.refs_4_), channel_id=1, source_target_pairs={{0,32},{8,40},{16,48},{24,56},{32,64},{40,72},{48,80},{56,88},{64,... | collective-permute-start | bytes 393224 | tf_op jit(solution)/shard_map/ppermute | solution.py:246
  13.9 8.2 %collective-permute-start.6 = (bf16[2,8,4096]{2,1,0:T(8,128)(2,1)S(1)}, bf16[2,8,4096]{2,1,0:T(8,128)(2,1)S(1)}, u32[]{:S(2)}, u32[]{:S(2)}) collective-permute-start(bf16[2,8,4096]{2,1,0:T(8,128)(2,1)S(1)} %pad_maximum_fusion.1.refs_4_), channel_id=1, source_target_pairs={{0,64},{8,72},{16,80},{24,88},{32,96},{40,104},{48,112},{56,120},{... | collective-permute-start | bytes 393224 | tf_op jit(solution)/shard_map/ppermute | solution.py:246
  16.4 7.3 %collective-permute-start.7 = (bf16[2,8,4096]{2,1,0:T(8,128)(2,1)S(1)}, bf16[2,8,4096]{2,1,0:T(8,128)(2,1)}, u32[]{:S(2)}, u32[]{:S(2)}) collective-permute-start(bf16[2,8,4096]{2,1,0:T(8,128)(2,1)S(1)} %pad_maximum_fusion.1.refs_4_), channel_id=1, source_target_pairs={{0,96},{8,104},{16,112},{24,120},{32,0},{40,8},{48,16},{56,24},{64... | collective-permute-start | bytes 393224 | tf_op jit(solution)/shard_map/ppermute | solution.py:246
  17.5 7.5 %collective-permute-start.3 = (bf16[2,16,2048]{2,1,0:T(8,128)(2,1)S(1)}, bf16[2,16,2048]{2,1,0:T(8,128)(2,1)S(1)}, u32[]{:S(2)}, u32[]{:S(2)}) collective-permute-start(bf16[2,16,2048]{2,1,0:T(8,128)(2,1)S(1)} %pad_maximum_fusion.refs_0_.l0), channel_id=1, source_target_pairs={{0,3},{1,0},{2,1},{3,2},{4,7},{5,4},{6,5},{7,6},{8,11},{9,8},{10,9... | collective-permute-start | bytes 393224 | tf_op jit(solution)/shard_map/ppermute | solution.py:244
  18.6 6.4 %collective-permute-start.8 = (bf16[2,8,4096]{2,1,0:T(8,128)(2,1)S(1)}, bf16[2,8,4096]{2,1,0:T(8,128)(2,1)}, u32[]{:S(2)}, u32[]{:S(2)}) collective-permute-start(bf16[2,8,4096]{2,1,0:T(8,128)(2,1)S(1)} %pad_maximum_fusion.1.refs_4_), channel_id=1, source_target_pairs={{0,8},{8,0},{16,24},{24,16},{32,40},{40,32},{48,56},{56,48},{64,72... | collective-permute-start | bytes 393224 | tf_op jit(solution)/shard_map/ppermute | solution.py:247
  21.5 3.5 %collective-permute-start.9 = (bf16[2,8,4096]{2,1,0:T(8,128)(2,1)S(1)}, bf16[2,8,4096]{2,1,0:T(8,128)(2,1)}, u32[]{:S(2)}, u32[]{:S(2)}) collective-permute-start(bf16[2,8,4096]{2,1,0:T(8,128)(2,1)S(1)} %collective-permute-done.5.refs_5_), channel_id=1, source_target_pairs={{0,8},{8,0},{16,24},{24,16},{32,40},{40,32},{48,56},{56,48},{64,72... | collective-permute-start | bytes 393224 | tf_op jit(solution)/shard_map/ppermute | solution.py:247
  22.1 3.0 %collective-permute-start.10 = (bf16[2,8,4096]{2,1,0:T(8,128)(2,1)S(1)}, bf16[2,8,4096]{2,1,0:T(8,128)(2,1)}, u32[]{:S(2)}, u32[]{:S(2)}) collective-permute-start(bf16[2,8,4096]{2,1,0:T(8,128)(2,1)S(1)} %collective-permute-done.6.refs_6_), channel_id=1, source_target_pairs={{0,8},{8,0},{16,24},{24,16},{32,40},{40,32},{48,56},{56,48},{64,72... | collective-permute-start | bytes 393224 | tf_op jit(solution)/shard_map/ppermute | solution.py:247
  23.6 1.7 %collective-permute-start.11 = (bf16[2,8,4096]{2,1,0:T(8,128)(2,1)}, bf16[2,8,4096]{2,1,0:T(8,128)(2,1)}, u32[]{:S(2)}, u32[]{:S(2)}) collective-permute-start(bf16[2,8,4096]{2,1,0:T(8,128)(2,1)} %collective-permute-done.7.refs_7_), channel_id=1, source_target_pairs={{0,8},{8,0},{16,24},{24,16},{32,40},{40,32},{48,56},{56,48},{64,72... | collective-permute-start | bytes 393224 | tf_op jit(solution)/shard_map/ppermute | solution.py:247
  40.1 1.2 %copy-start.1 = (bf16[4096,128]{1,0:T(8,128)(2,1)S(1)}, bf16[4096,128]{1,0:T(8,128)(2,1)}, u32[]{:S(2)}) copy-start(bf16[4096,128]{1,0:T(8,128)(2,1)} %get-tuple-element.19.rt_ref) | copy-start | bytes 3145732
  55.7 12.3 %copy-start.4 = (f32[8,8,4096]{2,1,0:T(8,128)S(1)}, f32[8,8,4096]{2,1,0:T(8,128)}, u32[]{:S(2)}) copy-start(f32[8,8,4096]{2,1,0:T(8,128)} %get-tuple-element.26) | copy-start | bytes 3145732
  55.7 11.3 %collective-permute-start.14 = (bf16[2,16,2048]{2,1,0:T(8,128)(2,1)}, bf16[2,16,2048]{2,1,0:T(8,128)(2,1)S(1)}, u32[]{:S(2)}, u32[]{:S(2)}) collective-permute-start(bf16[2,16,2048]{2,1,0:T(8,128)(2,1)} %get-tuple-element.25), channel_id=1, source_target_pairs={{0,3},{1,0},{2,1},{3,2},{4,7},{5,4},{6,5},{7,6},{8,11},{9,8},{10,9... | collective-permute-start | bytes 393224 | tf_op jit(solution)/shard_map/ppermute | solution.py:270
  56.8 10.2 %collective-permute-start.13 = (bf16[2,16,2048]{2,1,0:T(8,128)(2,1)}, bf16[2,16,2048]{2,1,0:T(8,128)(2,1)S(1)}, u32[]{:S(2)}, u32[]{:S(2)}) collective-permute-start(bf16[2,16,2048]{2,1,0:T(8,128)(2,1)} %get-tuple-element.24), channel_id=1, source_target_pairs={{0,2},{1,3},{2,0},{3,1},{4,6},{5,7},{6,4},{7,5},{8,10},{9,11},{10,... | collective-permute-start | bytes 393224 | tf_op jit(solution)/shard_map/ppermute | solution.py:270
  57.0 10.0 %collective-permute-start.12 = (bf16[2,16,2048]{2,1,0:T(8,128)(2,1)}, bf16[2,16,2048]{2,1,0:T(8,128)(2,1)S(1)}, u32[]{:S(2)}, u32[]{:S(2)}) collective-permute-start(bf16[2,16,2048]{2,1,0:T(8,128)(2,1)} %get-tuple-element.23), channel_id=1, source_target_pairs={{0,1},{1,2},{2,3},{3,0},{4,5},{5,6},{6,7},{7,4},{8,9},{9,10},{10,1... | collective-permute-start | bytes 393224 | tf_op jit(solution)/shard_map/ppermute | solution.py:270
  57.5 10.5 %collective-permute-start.16 = (bf16[8,8,4096]{2,1,0:T(8,128)(2,1)}, bf16[8,8,4096]{2,1,0:T(8,128)(2,1)S(1)}, u32[]{:S(2)}, u32[]{:S(2)}) collective-permute-start(bf16[8,8,4096]{2,1,0:T(8,128)(2,1)} %get-tuple-element.27), channel_id=1, source_target_pairs={{0,8},{8,0},{16,24},{24,16},{32,40},{40,32},{48,56},{56,48},{64,72... | collective-permute-start | bytes 1572872 | tf_op jit(solution)/shard_map/ppermute | solution.py:266
  59.1 22.2 %all-to-all-start = ((bf16[128,16,128]{2,1,0:T(8,128)(2,1)}), bf16[128,16,128]{2,1,0:T(8,128)(2,1)S(1)}, u32[]{:S(2)}, u32[]{:S(2)}) async-start(bf16[128,16,128]{2,1,0:T(8,128)(2,1)} %get-tuple-element.28), calls=%async_computation | async-start | bytes 1048576 | tf_op jit(solution)/shard_map/all_to_all | solution.py:256
  68.1 21.1 %collective-permute-start.19 = (bf16[2,8,4096]{2,1,0:T(8,128)(2,1)S(1)}, bf16[2,8,4096]{2,1,0:T(8,128)(2,1)S(1)}, u32[]{:S(2)}, u32[]{:S(2)}) collective-permute-start(bf16[2,8,4096]{2,1,0:T(8,128)(2,1)S(1)} %get-tuple-element.32), channel_id=1, source_target_pairs={{0,96},{8,104},{16,112},{24,120},{32,0},{40,8},{48,16},{56,24},{64... | collective-permute-start | bytes 393224 | tf_op jit(solution)/shard_map/ppermute | solution.py:269
  70.9 18.3 %collective-permute-start.18 = (bf16[2,8,4096]{2,1,0:T(8,128)(2,1)S(1)}, bf16[2,8,4096]{2,1,0:T(8,128)(2,1)S(1)}, u32[]{:S(2)}, u32[]{:S(2)}) collective-permute-start(bf16[2,8,4096]{2,1,0:T(8,128)(2,1)S(1)} %get-tuple-element.33), channel_id=1, source_target_pairs={{0,64},{8,72},{16,80},{24,88},{32,96},{40,104},{48,112},{56,120},{... | collective-permute-start | bytes 393224 | tf_op jit(solution)/shard_map/ppermute | solution.py:269
  71.5 17.7 %collective-permute-start.17 = (bf16[2,8,4096]{2,1,0:T(8,128)(2,1)S(1)}, bf16[2,8,4096]{2,1,0:T(8,128)(2,1)S(1)}, u32[]{:S(2)}, u32[]{:S(2)}) collective-permute-start(bf16[2,8,4096]{2,1,0:T(8,128)(2,1)S(1)} %get-tuple-element.31), channel_id=1, source_target_pairs={{0,32},{8,40},{16,48},{24,56},{32,64},{40,72},{48,80},{56,88},{64,... | collective-permute-start | bytes 393224 | tf_op jit(solution)/shard_map/ppermute | solution.py:269
  72.1 20.6 %collective-permute-start.15 = (bf16[16,2048]{1,0:T(8,128)(2,1)S(1)}, bf16[16,2048]{1,0:T(8,128)(2,1)S(1)}, u32[]{:S(2)}, u32[]{:S(2)}) collective-permute-start(bf16[16,2048]{1,0:T(8,128)(2,1)S(1)} %fusion.4), channel_id=1, source_target_pairs={{0,4},{1,5},{2,6},{3,7},{4,0},{5,1},{6,2},{7,3},{8,12},{9,13},{10,... | collective-permute-start | bytes 196616 | tf_op jit(solution)/shard_map/ppermute | solution.py:273
  81.3 0.8 copy-start.3
  84.1 19.0 %all-to-all-start.1 = ((f32[128,8,128]{2,1,0:T(8,128)}), f32[128,8,128]{2,1,0:T(8,128)S(1)}, u32[]{:S(2)}, u32[]{:S(2)}) async-start(f32[128,8,128]{2,1,0:T(8,128)} %get-tuple-element.29), calls=%async_computation.1 | async-start | bytes 1048576 | tf_op jit(solution)/shard_map/all_to_all | solution.py:263
  89.3 7.2 %collective-permute-start.20 = (bf16[8,4096]{1,0:T(8,128)(2,1)S(1)}, bf16[8,4096]{1,0:T(8,128)(2,1)S(1)}, u32[]{:S(2)}, u32[]{:S(2)}) collective-permute-start(bf16[8,4096]{1,0:T(8,128)(2,1)S(1)} %fusion.6), channel_id=1, source_target_pairs={{0,16},{8,24},{16,0},{24,8},{32,48},{40,56},{48,32},{56,40},{64,80... | collective-permute-start | bytes 196616 | tf_op jit(solution)/shard_map/ppermute | solution.py:276

commit v4 on v3

--- a/solution.py
+++ b/solution.py
@@ -110,7 +110,7 @@
 
 def weight_body(x_ref, gw_ref, gb_ref):
     total = jnp.sum(x_ref[...].astype(F32), axis=0)
-    gw_ref[...] = jnp.broadcast_to(total[None, :-8], gw_ref.shape)
+    gw_ref[...] = jnp.broadcast_to(total[None, :-8].astype(BF), gw_ref.shape)
     gb_ref[...] = jnp.sum(total[-8:], axis=0, keepdims=True)
 
 
@@ -257,10 +257,11 @@
     l0, l1, l2, l3, keep, send = backward(pieces, right_t, dpair, w)
     own, grad_b = pl.pallas_call(
         weight_body,
-        out_shape=(pltpu.HBM((ndev, CL * CL // ndev, CP), F32), jax.ShapeDtypeStruct((1, CP), F32)),
+        out_shape=(pltpu.HBM((ndev, CL * CL // ndev, CP), BF), jax.ShapeDtypeStruct((1, CP), F32)),
         name="weight",
     )(share)
-    grad_w = lax.all_to_all(own, ("row", "col"), 0, 0, tiled=True).reshape(CL * CL, CP)
+    grad_w = lax.all_to_all(own, ("row", "col"), 0, 0, tiled=True)
+    grad_w = grad_w.reshape(CL * CL, CP).astype(F32)
     grad_b = grad_b.reshape(CP)
 
     got = lax.ppermute(send, "row", row_shift(0, 0, 1))

time: 104 us -> 102 us (0.981)
  waiting for transfers between devices: 16.8 us -> 14.1 us
    ppermute x1, waiting for transfers between devices: 3.19 us -> 1.51 us  [shards(): rz = lax.ppermute(rfar, 'row', row_shift(0, 1, 0))]
    all_to_all x1, waiting for transfers between devices: 5.52 us -> 4.48 us  [shards(): grad_w = lax.all_to_all(own, ('row', 'col'), 0, 0, tiled=True)]
    unnamed x11 -> x10, local copies, waits for them, and re-layouts: 2.82 us -> 2.03 us
where the time goes in v4:
time: 102 us; the launch traced here: 101 us
  starting transfers between devices  46.1 us (45%)
  Pallas kernels  31 us (30%)
  waiting for transfers between devices  14.1 us (14%)
  local copies, waits for them, and re-layouts  5.55 us (5%)
  other arithmetic  3.51 us (3%)
    pallas_call x1, Pallas kernels, forward(): pl.pallas_call(forward_body, grid=(n,), out_shape=(jax.ShapeDtypeStruct((...  14.7 us
    pallas_call x1, Pallas kernels, backward(): pl.pallas_call(backward_body, grid=(n,), out_shape=(pltpu.HBM((NZ, scol,...  14.4 us
    all_to_all x1, starting transfers between devices, shards(): share = lax.all_to_all(share, ('row', 'col'), 0, 0, tiled=True)  7.83 us
    all_to_all x1, waiting for transfers between devices, shards(): share = lax.all_to_all(share, ('row', 'col'), 0, 0, tiled=True)  7.81 us
    ppermute x4, starting transfers between devices, shards(): theirs = [lax.ppermute(p, 'row', row_shift(0, 0, 1)) for p in mine]  5.19 us
    all_to_all x1, starting transfers between devices, shards(): grad_w = lax.all_to_all(own, ('row', 'col'), 0, 0, tiled=True)  5.07 us
    ppermute x3, starting transfers between devices, shards(): lax.ppermute(pair, 'col', col_shift(0, d))  5.05 us
    ppermute x3, starting transfers between devices, shards(): lax.ppermute(pair, 'row', row_shift(d, 0, 0))  4.88 us
  transfers between devices with their start and end apart: 23, of which 4 were waited for; matrix products, arithmetic and copies ran while one was open for 6% of the time, Pallas kernels for 2%

profile of v4, /device:TPU:1, one launch (start us, length us, event | category | flops | bytes accessed | tf_op | source)
XLA Modules:
  0.0 101.1 jit_solution(13800240401617082155)
XLA Ops:
  0.7 2.5 %collective-permute-start = (bf16[16,2048]{1,0:T(8,128)(2,1)}, bf16[16,2048]{1,0:T(8,128)(2,1)S(1)}, u32[]{:S(2)}, u32[]{:S(2)}) collective-permute-start(bf16[16,2048]{1,0:T(8,128)(2,1)} %param.5), channel_id=1, source_target_pairs={{0,4},{1,5},{2,6},{3,7},{4,0},{5,1},{6,2},{7,3},{8,12},{9,13},{10,... | collective-permute-start | bytes 196616 | tf_op jit(solution)/shard_map/ppermute | solution.py:240
  3.2 1.1 %reshape.45 = bf16[8,128,32]{2,1,0:T(8,128)(2,1)S(1)} reshape(bf16[8,4096]{1,0:T(8,128)(2,1)} %param.6) | data formatting | bytes 131072 | tf_op jit(solution)/shard_map/reshape | solution.py:241
  4.4 3.4 %collective-permute-start.4 = (bf16[8,4096]{1,0:T(8,128)(2,1)S(1)}, bf16[8,4096]{1,0:T(8,128)(2,1)S(1)}, u32[]{:S(2)}, u32[]{:S(2)}) collective-permute-start(bf16[8,4096]{1,0:T(8,128)(2,1)S(1)} %bitcast.48), channel_id=1, source_target_pairs={{0,16},{8,24},{16,0},{24,8},{32,48},{40,56},{48,32},{56,40},{64,80... | collective-permute-start | bytes 196616 | tf_op jit(solution)/shard_map/ppermute | solution.py:242
  7.8 0.9 pad_maximum_fusion.refs_0_.l0
  8.6 1.4 %collective-permute-start.1 = (bf16[2,16,2048]{2,1,0:T(8,128)(2,1)S(1)}, bf16[2,16,2048]{2,1,0:T(8,128)(2,1)S(1)}, u32[]{:S(2)}, u32[]{:S(2)}) collective-permute-start(bf16[2,16,2048]{2,1,0:T(8,128)(2,1)S(1)} %pad_maximum_fusion.refs_0_.l0), channel_id=1, source_target_pairs={{0,1},{1,2},{2,3},{3,0},{4,5},{5,6},{6,7},{7,4},{8,9},{9,10},{10,1... | collective-permute-start | bytes 393224 | tf_op jit(solution)/shard_map/ppermute | solution.py:244
  10.0 2.6 %collective-permute-start.2 = (bf16[2,16,2048]{2,1,0:T(8,128)(2,1)S(1)}, bf16[2,16,2048]{2,1,0:T(8,128)(2,1)S(1)}, u32[]{:S(2)}, u32[]{:S(2)}) collective-permute-start(bf16[2,16,2048]{2,1,0:T(8,128)(2,1)S(1)} %pad_maximum_fusion.refs_0_.l0), channel_id=1, source_target_pairs={{0,2},{1,3},{2,0},{3,1},{4,6},{5,7},{6,4},{7,5},{8,10},{9,11},{10,... | collective-permute-start | bytes 393224 | tf_op jit(solution)/shard_map/ppermute | solution.py:244
  12.7 1.3 %collective-permute-start.5 = (bf16[2,8,4096]{2,1,0:T(8,128)(2,1)S(1)}, bf16[2,8,4096]{2,1,0:T(8,128)(2,1)S(1)}, u32[]{:S(2)}, u32[]{:S(2)}) collective-permute-start(bf16[2,8,4096]{2,1,0:T(8,128)(2,1)S(1)} %pad_maximum_fusion.1.refs_4_), channel_id=1, source_target_pairs={{0,32},{8,40},{16,48},{24,56},{32,64},{40,72},{48,80},{56,88},{64,... | collective-permute-start | bytes 393224 | tf_op jit(solution)/shard_map/ppermute | solution.py:246
  13.9 2.5 %collective-permute-start.6 = (bf16[2,8,4096]{2,1,0:T(8,128)(2,1)S(1)}, bf16[2,8,4096]{2,1,0:T(8,128)(2,1)S(1)}, u32[]{:S(2)}, u32[]{:S(2)}) collective-permute-start(bf16[2,8,4096]{2,1,0:T(8,128)(2,1)S(1)} %pad_maximum_fusion.1.refs_4_), channel_id=1, source_target_pairs={{0,64},{8,72},{16,80},{24,88},{32,96},{40,104},{48,112},{56,120},{... | collective-permute-start | bytes 393224 | tf_op jit(solution)/shard_map/ppermute | solution.py:246
  16.4 1.2 %collective-permute-start.7 = (bf16[2,8,4096]{2,1,0:T(8,128)(2,1)S(1)}, bf16[2,8,4096]{2,1,0:T(8,128)(2,1)}, u32[]{:S(2)}, u32[]{:S(2)}) collective-permute-start(bf16[2,8,4096]{2,1,0:T(8,128)(2,1)S(1)} %pad_maximum_fusion.1.refs_4_), channel_id=1, source_target_pairs={{0,96},{8,104},{16,112},{24,120},{32,0},{40,8},{48,16},{56,24},{64... | collective-permute-start | bytes 393224 | tf_op jit(solution)/shard_map/ppermute | solution.py:246
  17.5 1.1 %collective-permute-start.3 = (bf16[2,16,2048]{2,1,0:T(8,128)(2,1)S(1)}, bf16[2,16,2048]{2,1,0:T(8,128)(2,1)S(1)}, u32[]{:S(2)}, u32[]{:S(2)}) collective-permute-start(bf16[2,16,2048]{2,1,0:T(8,128)(2,1)S(1)} %pad_maximum_fusion.refs_0_.l0), channel_id=1, source_target_pairs={{0,3},{1,0},{2,1},{3,2},{4,7},{5,4},{6,5},{7,6},{8,11},{9,8},{10,9... | collective-permute-start | bytes 393224 | tf_op jit(solution)/shard_map/ppermute | solution.py:244
  18.6 2.9 %collective-permute-start.8 = (bf16[2,8,4096]{2,1,0:T(8,128)(2,1)S(1)}, bf16[2,8,4096]{2,1,0:T(8,128)(2,1)}, u32[]{:S(2)}, u32[]{:S(2)}) collective-permute-start(bf16[2,8,4096]{2,1,0:T(8,128)(2,1)S(1)} %pad_maximum_fusion.1.refs_4_), channel_id=1, source_target_pairs={{0,8},{8,0},{16,24},{24,16},{32,40},{40,32},{48,56},{56,48},{64,72... | collective-permute-start | bytes 393224 | tf_op jit(solution)/shard_map/ppermute | solution.py:247
  22.1 1.5 %collective-permute-start.10 = (bf16[2,8,4096]{2,1,0:T(8,128)(2,1)S(1)}, bf16[2,8,4096]{2,1,0:T(8,128)(2,1)}, u32[]{:S(2)}, u32[]{:S(2)}) collective-permute-start(bf16[2,8,4096]{2,1,0:T(8,128)(2,1)S(1)} %collective-permute-done.6.refs_6_), channel_id=1, source_target_pairs={{0,8},{8,0},{16,24},{24,16},{32,40},{40,32},{48,56},{56,48},{64,72... | collective-permute-start | bytes 393224 | tf_op jit(solution)/shard_map/ppermute | solution.py:247
  23.8 1.1 %copy.16 = bf16[32,32,128]{2,0,1:T(8,128)(2,1)S(1)} copy(bf16[32,32,128]{2,1,0:T(8,128)(2,1)} %bitcast.47) | data formatting | bytes 524288 | tf_op jit(solution)/shard_map/reshape | solution.py:250
  25.3 14.7 %forward.1 = (bf16[8192,128]{1,0:T(8,128)(2,1)}, bf16[128,16,128]{2,1,0:T(8,128)(2,1)}, bf16[4096,128]{1,0:T(8,128)(2,1)}) custom-call(bf16[2,16,2048]{2,1,0:T(8,128)(2,1)S(1)} %pad_maximum_fusion.refs_0_.l0, bf16[2,16,2048]{2,1,0:T(8,128)(2,1)S(1)} %collective-permute-done.1.refs_1_.l1, bf16[2,16,2048]{2,1,0:T(8,128)(2,1)S(1)} %collective-permute-done.2.refs_2_.l2, ...), custom_call_target="tpu_custom_call" | custom-call | tf_op jit(solution)/shard_map/forward/pallas_call | solution.py:169
  40.1 1.2 %copy-done.1 = bf16[4096,128]{1,0:T(8,128)(2,1)S(1)} copy-done((bf16[4096,128]{1,0:T(8,128)(2,1)S(1)}, bf16[4096,128]{1,0:T(8,128)(2,1)}, u32[]{:S(2)}) %copy-start.1) | copy-done | bytes 1048600
  41.3 14.4 %backward.1 = (f32[2,16,2048]{2,1,0:T(8,128)}, bf16[2,16,2048]{2,1,0:T(8,128)(2,1)}, bf16[2,16,2048]{2,1,0:T(8,128)(2,1)}, bf16[2,16,2048]{2,1,0:T(8,128)(2,1)},...) custom-call(bf16[2,16,2048]{2,1,0:T(8,128)(2,1)S(1)} %pad_maximum_fusion.refs_0_.l0, ...), custom_call_target="tpu_custom_call" | custom-call | tf_op jit(solution)/shard_map/backward/pallas_call | solution.py:207
  55.7 1.1 %collective-permute-start.14 = (bf16[2,16,2048]{2,1,0:T(8,128)(2,1)}, bf16[2,16,2048]{2,1,0:T(8,128)(2,1)S(1)}, u32[]{:S(2)}, u32[]{:S(2)}) collective-permute-start(bf16[2,16,2048]{2,1,0:T(8,128)(2,1)} %get-tuple-element.25), channel_id=1, source_target_pairs={{0,3},{1,0},{2,1},{3,2},{4,7},{5,4},{6,5},{7,6},{8,11},{9,8},{10,9... | collective-permute-start | bytes 393224 | tf_op jit(solution)/shard_map/ppermute | solution.py:271
  57.5 1.6 %collective-permute-start.16 = (bf16[8,8,4096]{2,1,0:T(8,128)(2,1)}, bf16[8,8,4096]{2,1,0:T(8,128)(2,1)S(1)}, u32[]{:S(2)}, u32[]{:S(2)}) collective-permute-start(bf16[8,8,4096]{2,1,0:T(8,128)(2,1)} %get-tuple-element.27), channel_id=1, source_target_pairs={{0,8},{8,0},{16,24},{24,16},{32,40},{40,32},{48,56},{56,48},{64,72... | collective-permute-start | bytes 1572872 | tf_op jit(solution)/shard_map/ppermute | solution.py:267
  59.1 7.8 %all-to-all-start = ((bf16[128,16,128]{2,1,0:T(8,128)(2,1)}), bf16[128,16,128]{2,1,0:T(8,128)(2,1)S(1)}, u32[]{:S(2)}, u32[]{:S(2)}) async-start(bf16[128,16,128]{2,1,0:T(8,128)(2,1)} %get-tuple-element.28), calls=%async_computation | async-start | bytes 1048576 | tf_op jit(solution)/shard_map/all_to_all | solution.py:256
  67.0 1.0 add_add_fusion.1
  68.1 2.8 %collective-permute-start.19 = (bf16[2,8,4096]{2,1,0:T(8,128)(2,1)S(1)}, bf16[2,8,4096]{2,1,0:T(8,128)(2,1)S(1)}, u32[]{:S(2)}, u32[]{:S(2)}) collective-permute-start(bf16[2,8,4096]{2,1,0:T(8,128)(2,1)S(1)} %get-tuple-element.32), channel_id=1, source_target_pairs={{0,96},{8,104},{16,112},{24,120},{32,0},{40,8},{48,16},{56,24},{64... | collective-permute-start | bytes 393224 | tf_op jit(solution)/shard_map/ppermute | solution.py:270
  72.1 1.4 %collective-permute-start.15 = (bf16[16,2048]{1,0:T(8,128)(2,1)S(1)}, bf16[16,2048]{1,0:T(8,128)(2,1)S(1)}, u32[]{:S(2)}, u32[]{:S(2)}) collective-permute-start(bf16[16,2048]{1,0:T(8,128)(2,1)S(1)} %fusion.4), channel_id=1, source_target_pairs={{0,4},{1,5},{2,6},{3,7},{4,0},{5,1},{6,2},{7,3},{8,12},{9,13},{10,... | collective-permute-start | bytes 196616 | tf_op jit(solution)/shard_map/ppermute | solution.py:274
  73.5 7.8 %all-to-all-done.x_ref = bf16[128,16,128]{2,1,0:T(8,128)(2,1)S(1)} async-done(((bf16[128,16,128]{2,1,0:T(8,128)(2,1)}), bf16[128,16,128]{2,1,0:T(8,128)(2,1)S(1)}, u32[]{:S(2)}, u32[]{:S(2)}) %all-to-all-start) | async-done | bytes 524320 | tf_op jit(solution)/shard_map/all_to_all | solution.py:256
  81.3 0.8 copy-done.3
  82.1 1.9 %weight.1 = (bf16[128,8,128]{2,1,0:T(8,128)(2,1)}, f32[1,128]{1,0:T(1,128)}) custom-call(bf16[128,16,128]{2,1,0:T(8,128)(2,1)} %copy-done.3), custom_call_target="tpu_custom_call" | custom-call | tf_op jit(solution)/shard_map/weight/pallas_call | solution.py:258
  84.0 5.1 %all-to-all-start.1 = ((bf16[128,8,128]{2,1,0:T(8,128)(2,1)}), bf16[128,8,128]{2,1,0:T(8,128)(2,1)S(1)}, u32[]{:S(2)}, u32[]{:S(2)}) async-start(bf16[128,8,128]{2,1,0:T(8,128)(2,1)} %get-tuple-element.29), calls=%async_computation.1 | async-start | bytes 524288 | tf_op jit(solution)/shard_map/all_to_all | solution.py:263
  89.2 3.3 %collective-permute-start.20 = (bf16[8,4096]{1,0:T(8,128)(2,1)S(1)}, bf16[8,4096]{1,0:T(8,128)(2,1)S(1)}, u32[]{:S(2)}, u32[]{:S(2)}) collective-permute-start(bf16[8,4096]{1,0:T(8,128)(2,1)S(1)} %fusion.6), channel_id=1, source_target_pairs={{0,16},{8,24},{16,0},{24,8},{32,48},{40,56},{48,32},{56,40},{64,80... | collective-permute-start | bytes 196616 | tf_op jit(solution)/shard_map/ppermute | solution.py:277
  92.5 0.6 fusion.3
  93.2 1.5 %collective-permute-done.20 = bf16[8,4096]{1,0:T(8,128)(2,1)S(1)} collective-permute-done((bf16[8,4096]{1,0:T(8,128)(2,1)S(1)}, bf16[8,4096]{1,0:T(8,128)(2,1)S(1)}, u32[]{:S(2)}, u32[]{:S(2)}) %collective-permute-start.20) | collective-permute-done | bytes 65568 | tf_op jit(solution)/shard_map/ppermute | solution.py:277
  94.9 0.9 reshape.53
  95.8 4.5 %all-to-all-done.1 = bf16[128,8,128]{2,1,0:T(8,128)(2,1)S(1)} async-done(((bf16[128,8,128]{2,1,0:T(8,128)(2,1)}), bf16[128,8,128]{2,1,0:T(8,128)(2,1)S(1)}, u32[]{:S(2)}, u32[]{:S(2)}) %all-to-all-start.1) | async-done | bytes 262176 | tf_op jit(solution)/shard_map/all_to_all | solution.py:263
  100.3 0.8 bitcast_convert_fusion
  (43 shorter events, 3.6 us)
Async XLA Ops:
  0.6 24.7 %copy-start = (bf16[64,128,128]{2,1,0:T(8,128)(2,1)S(1)}, bf16[64,128,128]{2,1,0:T(8,128)(2,1)}, u32[]{:S(2)}) copy-start(bf16[64,128,128]{2,1,0:T(8,128)(2,1)} %param.9) | copy-start | bytes 6291460
  0.6 24.7 %copy-start.2 = (f32[128]{0:T(128)S(1)}, f32[128]{0:T(128)}, u32[]{:S(2)}) copy-start(f32[128]{0:T(128)} %param.8) | copy-start | bytes 1540
  0.7 7.1 %collective-permute-start = (bf16[16,2048]{1,0:T(8,128)(2,1)}, bf16[16,2048]{1,0:T(8,128)(2,1)S(1)}, u32[]{:S(2)}, u32[]{:S(2)}) collective-permute-start(bf16[16,2048]{1,0:T(8,128)(2,1)} %param.5), channel_id=1, source_target_pairs={{0,4},{1,5},{2,6},{3,7},{4,0},{5,1},{6,2},{7,3},{8,12},{9,13},{10,... | collective-permute-start | bytes 196616 | tf_op jit(solution)/shard_map/ppermute | solution.py:240
  4.4 8.2 %collective-permute-start.4 = (bf16[8,4096]{1,0:T(8,128)(2,1)S(1)}, bf16[8,4096]{1,0:T(8,128)(2,1)S(1)}, u32[]{:S(2)}, u32[]{:S(2)}) collective-permute-start(bf16[8,4096]{1,0:T(8,128)(2,1)S(1)} %bitcast.48), channel_id=1, source_target_pairs={{0,16},{8,24},{16,0},{24,8},{32,48},{40,56},{48,32},{56,40},{64,80... | collective-permute-start | bytes 196616 | tf_op jit(solution)/shard_map/ppermute | solution.py:242
  8.6 8.9 %collective-permute-start.1 = (bf16[2,16,2048]{2,1,0:T(8,128)(2,1)S(1)}, bf16[2,16,2048]{2,1,0:T(8,128)(2,1)S(1)}, u32[]{:S(2)}, u32[]{:S(2)}) collective-permute-start(bf16[2,16,2048]{2,1,0:T(8,128)(2,1)S(1)} %pad_maximum_fusion.refs_0_.l0), channel_id=1, source_target_pairs={{0,1},{1,2},{2,3},{3,0},{4,5},{5,6},{6,7},{7,4},{8,9},{9,10},{10,1... | collective-permute-start | bytes 393224 | tf_op jit(solution)/shard_map/ppermute | solution.py:244
  10.0 8.6 %collective-permute-start.2 = (bf16[2,16,2048]{2,1,0:T(8,128)(2,1)S(1)}, bf16[2,16,2048]{2,1,0:T(8,128)(2,1)S(1)}, u32[]{:S(2)}, u32[]{:S(2)}) collective-permute-start(bf16[2,16,2048]{2,1,0:T(8,128)(2,1)S(1)} %pad_maximum_fusion.refs_0_.l0), channel_id=1, source_target_pairs={{0,2},{1,3},{2,0},{3,1},{4,6},{5,7},{6,4},{7,5},{8,10},{9,11},{10,... | collective-permute-start | bytes 393224 | tf_op jit(solution)/shard_map/ppermute | solution.py:244
  12.7 8.9 %collective-permute-start.5 = (bf16[2,8,4096]{2,1,0:T(8,128)(2,1)S(1)}, bf16[2,8,4096]{2,1,0:T(8,128)(2,1)S(1)}, u32[]{:S(2)}, u32[]{:S(2)}) collective-permute-start(bf16[2,8,4096]{2,1,0:T(8,128)(2,1)S(1)} %pad_maximum_fusion.1.refs_4_), channel_id=1, source_target_pairs={{0,32},{8,40},{16,48},{24,56},{32,64},{40,72},{48,80},{56,88},{64,... | collective-permute-start | bytes 393224 | tf_op jit(solution)/shard_map/ppermute | solution.py:246
  13.9 8.2 %collective-permute-start.6 = (bf16[2,8,4096]{2,1,0:T(8,128)(2,1)S(1)}, bf16[2,8,4096]{2,1,0:T(8,128)(2,1)S(1)}, u32[]{:S(2)}, u32[]{:S(2)}) collective-permute-start(bf16[2,8,4096]{2,1,0:T(8,128)(2,1)S(1)} %pad_maximum_fusion.1.refs_4_), channel_id=1, source_target_pairs={{0,64},{8,72},{16,80},{24,88},{32,96},{40,104},{48,112},{56,120},{... | collective-permute-start | bytes 393224 | tf_op jit(solution)/shard_map/ppermute | solution.py:246
  16.4 7.3 %collective-permute-start.7 = (bf16[2,8,4096]{2,1,0:T(8,128)(2,1)S(1)}, bf16[2,8,4096]{2,1,0:T(8,128)(2,1)}, u32[]{:S(2)}, u32[]{:S(2)}) collective-permute-start(bf16[2,8,4096]{2,1,0:T(8,128)(2,1)S(1)} %pad_maximum_fusion.1.refs_4_), channel_id=1, source_target_pairs={{0,96},{8,104},{16,112},{24,120},{32,0},{40,8},{48,16},{56,24},{64... | collective-permute-start | bytes 393224 | tf_op jit(solution)/shard_map/ppermute | solution.py:246
  17.5 7.5 %collective-permute-start.3 = (bf16[2,16,2048]{2,1,0:T(8,128)(2,1)S(1)}, bf16[2,16,2048]{2,1,0:T(8,128)(2,1)S(1)}, u32[]{:S(2)}, u32[]{:S(2)}) collective-permute-start(bf16[2,16,2048]{2,1,0:T(8,128)(2,1)S(1)} %pad_maximum_fusion.refs_0_.l0), channel_id=1, source_target_pairs={{0,3},{1,0},{2,1},{3,2},{4,7},{5,4},{6,5},{7,6},{8,11},{9,8},{10,9... | collective-permute-start | bytes 393224 | tf_op jit(solution)/shard_map/ppermute | solution.py:244
  18.6 6.4 %collective-permute-start.8 = (bf16[2,8,4096]{2,1,0:T(8,128)(2,1)S(1)}, bf16[2,8,4096]{2,1,0:T(8,128)(2,1)}, u32[]{:S(2)}, u32[]{:S(2)}) collective-permute-start(bf16[2,8,4096]{2,1,0:T(8,128)(2,1)S(1)} %pad_maximum_fusion.1.refs_4_), channel_id=1, source_target_pairs={{0,8},{8,0},{16,24},{24,16},{32,40},{40,32},{48,56},{56,48},{64,72... | collective-permute-start | bytes 393224 | tf_op jit(solution)/shard_map/ppermute | solution.py:247
  21.5 3.5 %collective-permute-start.9 = (bf16[2,8,4096]{2,1,0:T(8,128)(2,1)S(1)}, bf16[2,8,4096]{2,1,0:T(8,128)(2,1)}, u32[]{:S(2)}, u32[]{:S(2)}) collective-permute-start(bf16[2,8,4096]{2,1,0:T(8,128)(2,1)S(1)} %collective-permute-done.5.refs_5_), channel_id=1, source_target_pairs={{0,8},{8,0},{16,24},{24,16},{32,40},{40,32},{48,56},{56,48},{64,72... | collective-permute-start | bytes 393224 | tf_op jit(solution)/shard_map/ppermute | solution.py:247
  22.1 3.0 %collective-permute-start.10 = (bf16[2,8,4096]{2,1,0:T(8,128)(2,1)S(1)}, bf16[2,8,4096]{2,1,0:T(8,128)(2,1)}, u32[]{:S(2)}, u32[]{:S(2)}) collective-permute-start(bf16[2,8,4096]{2,1,0:T(8,128)(2,1)S(1)} %collective-permute-done.6.refs_6_), channel_id=1, source_target_pairs={{0,8},{8,0},{16,24},{24,16},{32,40},{40,32},{48,56},{56,48},{64,72... | collective-permute-start | bytes 393224 | tf_op jit(solution)/shard_map/ppermute | solution.py:247
  23.6 1.7 %collective-permute-start.11 = (bf16[2,8,4096]{2,1,0:T(8,128)(2,1)}, bf16[2,8,4096]{2,1,0:T(8,128)(2,1)}, u32[]{:S(2)}, u32[]{:S(2)}) collective-permute-start(bf16[2,8,4096]{2,1,0:T(8,128)(2,1)} %collective-permute-done.7.refs_7_), channel_id=1, source_target_pairs={{0,8},{8,0},{16,24},{24,16},{32,40},{40,32},{48,56},{56,48},{64,72... | collective-permute-start | bytes 393224 | tf_op jit(solution)/shard_map/ppermute | solution.py:247
  40.1 1.2 %copy-start.1 = (bf16[4096,128]{1,0:T(8,128)(2,1)S(1)}, bf16[4096,128]{1,0:T(8,128)(2,1)}, u32[]{:S(2)}) copy-start(bf16[4096,128]{1,0:T(8,128)(2,1)} %get-tuple-element.19.rt_ref) | copy-start | bytes 3145732
  55.7 12.3 %copy-start.4 = (f32[8,8,4096]{2,1,0:T(8,128)S(1)}, f32[8,8,4096]{2,1,0:T(8,128)}, u32[]{:S(2)}) copy-start(f32[8,8,4096]{2,1,0:T(8,128)} %get-tuple-element.26) | copy-start | bytes 3145732
  55.7 11.3 %collective-permute-start.14 = (bf16[2,16,2048]{2,1,0:T(8,128)(2,1)}, bf16[2,16,2048]{2,1,0:T(8,128)(2,1)S(1)}, u32[]{:S(2)}, u32[]{:S(2)}) collective-permute-start(bf16[2,16,2048]{2,1,0:T(8,128)(2,1)} %get-tuple-element.25), channel_id=1, source_target_pairs={{0,3},{1,0},{2,1},{3,2},{4,7},{5,4},{6,5},{7,6},{8,11},{9,8},{10,9... | collective-permute-start | bytes 393224 | tf_op jit(solution)/shard_map/ppermute | solution.py:271
  56.8 10.2 %collective-permute-start.13 = (bf16[2,16,2048]{2,1,0:T(8,128)(2,1)}, bf16[2,16,2048]{2,1,0:T(8,128)(2,1)S(1)}, u32[]{:S(2)}, u32[]{:S(2)}) collective-permute-start(bf16[2,16,2048]{2,1,0:T(8,128)(2,1)} %get-tuple-element.24), channel_id=1, source_target_pairs={{0,2},{1,3},{2,0},{3,1},{4,6},{5,7},{6,4},{7,5},{8,10},{9,11},{10,... | collective-permute-start | bytes 393224 | tf_op jit(solution)/shard_map/ppermute | solution.py:271
  57.0 10.0 %collective-permute-start.12 = (bf16[2,16,2048]{2,1,0:T(8,128)(2,1)}, bf16[2,16,2048]{2,1,0:T(8,128)(2,1)S(1)}, u32[]{:S(2)}, u32[]{:S(2)}) collective-permute-start(bf16[2,16,2048]{2,1,0:T(8,128)(2,1)} %get-tuple-element.23), channel_id=1, source_target_pairs={{0,1},{1,2},{2,3},{3,0},{4,5},{5,6},{6,7},{7,4},{8,9},{9,10},{10,1... | collective-permute-start | bytes 393224 | tf_op jit(solution)/shard_map/ppermute | solution.py:271
  57.5 10.5 %collective-permute-start.16 = (bf16[8,8,4096]{2,1,0:T(8,128)(2,1)}, bf16[8,8,4096]{2,1,0:T(8,128)(2,1)S(1)}, u32[]{:S(2)}, u32[]{:S(2)}) collective-permute-start(bf16[8,8,4096]{2,1,0:T(8,128)(2,1)} %get-tuple-element.27), channel_id=1, source_target_pairs={{0,8},{8,0},{16,24},{24,16},{32,40},{40,32},{48,56},{56,48},{64,72... | collective-permute-start | bytes 1572872 | tf_op jit(solution)/shard_map/ppermute | solution.py:267
  59.1 22.2 %all-to-all-start = ((bf16[128,16,128]{2,1,0:T(8,128)(2,1)}), bf16[128,16,128]{2,1,0:T(8,128)(2,1)S(1)}, u32[]{:S(2)}, u32[]{:S(2)}) async-start(bf16[128,16,128]{2,1,0:T(8,128)(2,1)} %get-tuple-element.28), calls=%async_computation | async-start | bytes 1048576 | tf_op jit(solution)/shard_map/all_to_all | solution.py:256
  68.1 21.0 %collective-permute-start.19 = (bf16[2,8,4096]{2,1,0:T(8,128)(2,1)S(1)}, bf16[2,8,4096]{2,1,0:T(8,128)(2,1)S(1)}, u32[]{:S(2)}, u32[]{:S(2)}) collective-permute-start(bf16[2,8,4096]{2,1,0:T(8,128)(2,1)S(1)} %get-tuple-element.32), channel_id=1, source_target_pairs={{0,96},{8,104},{16,112},{24,120},{32,0},{40,8},{48,16},{56,24},{64... | collective-permute-start | bytes 393224 | tf_op jit(solution)/shard_map/ppermute | solution.py:270
  70.9 18.2 %collective-permute-start.18 = (bf16[2,8,4096]{2,1,0:T(8,128)(2,1)S(1)}, bf16[2,8,4096]{2,1,0:T(8,128)(2,1)S(1)}, u32[]{:S(2)}, u32[]{:S(2)}) collective-permute-start(bf16[2,8,4096]{2,1,0:T(8,128)(2,1)S(1)} %get-tuple-element.33), channel_id=1, source_target_pairs={{0,64},{8,72},{16,80},{24,88},{32,96},{40,104},{48,112},{56,120},{... | collective-permute-start | bytes 393224 | tf_op jit(solution)/shard_map/ppermute | solution.py:270
  71.5 17.6 %collective-permute-start.17 = (bf16[2,8,4096]{2,1,0:T(8,128)(2,1)S(1)}, bf16[2,8,4096]{2,1,0:T(8,128)(2,1)S(1)}, u32[]{:S(2)}, u32[]{:S(2)}) collective-permute-start(bf16[2,8,4096]{2,1,0:T(8,128)(2,1)S(1)} %get-tuple-element.31), channel_id=1, source_target_pairs={{0,32},{8,40},{16,48},{24,56},{32,64},{40,72},{48,80},{56,88},{64,... | collective-permute-start | bytes 393224 | tf_op jit(solution)/shard_map/ppermute | solution.py:270
  72.1 20.5 %collective-permute-start.15 = (bf16[16,2048]{1,0:T(8,128)(2,1)S(1)}, bf16[16,2048]{1,0:T(8,128)(2,1)S(1)}, u32[]{:S(2)}, u32[]{:S(2)}) collective-permute-start(bf16[16,2048]{1,0:T(8,128)(2,1)S(1)} %fusion.4), channel_id=1, source_target_pairs={{0,4},{1,5},{2,6},{3,7},{4,0},{5,1},{6,2},{7,3},{8,12},{9,13},{10,... | collective-permute-start | bytes 196616 | tf_op jit(solution)/shard_map/ppermute | solution.py:274
  81.3 0.8 copy-start.3
  84.0 16.3 %all-to-all-start.1 = ((bf16[128,8,128]{2,1,0:T(8,128)(2,1)}), bf16[128,8,128]{2,1,0:T(8,128)(2,1)S(1)}, u32[]{:S(2)}, u32[]{:S(2)}) async-start(bf16[128,8,128]{2,1,0:T(8,128)(2,1)} %get-tuple-element.29), calls=%async_computation.1 | async-start | bytes 524288 | tf_op jit(solution)/shard_map/all_to_all | solution.py:263
  89.2 5.5 %collective-permute-start.20 = (bf16[8,4096]{1,0:T(8,128)(2,1)S(1)}, bf16[8,4096]{1,0:T(8,128)(2,1)S(1)}, u32[]{:S(2)}, u32[]{:S(2)}) collective-permute-start(bf16[8,4096]{1,0:T(8,128)(2,1)S(1)} %fusion.6), channel_id=1, source_target_pairs={{0,16},{8,24},{16,0},{24,8},{32,48},{40,56},{48,32},{56,40},{64,80... | collective-permute-start | bytes 196616 | tf_op jit(solution)/shard_map/ppermute | solution.py:277
